TPU v7x, 512 devices: a whole 4x8x8 slice. The times are simulated.
512 devices in a mesh: row: 32 (over z, x), col: 16 (over y, core).
Axes of the slice: x: 4, y: 8, z: 8, core: 2. Of those that a mesh axis runs over, the one named last changes fastest.
Arguments:
- covariance: float32 [2, 4096, 4, 2048], P(None, 'row', None, 'col'), may hold values from -0.05 to 24.05, as said below
Outputs:
- factored: float32 [2, 4096, 4, 2048], P(None, 'row', None, 'col')
Inputs may be any that keep to these rules, and one draw needn't show every extreme that they name: covariance holds a symmetric matrix whose leading principal block of order 3 * 128 is positive definite.
All inputs are finite; a program needn't handle non-finite values.
Results may differ from a plain program's by a relative error of at most 0.0002.
Values sent between devices are 32-bit elements; how exact they have to be, the bound alone decides.
No kernel may reach another device: no remote copies, remote signals or barrier semaphores. Data moves between devices by JAX's collectives and lax.ppermute only.
A program may use at most 64 MiB of HBM per device.

v0:
```python
import jax
import jax.numpy as jnp
from jax import lax
from jax.sharding import PartitionSpec as P

PANELS = 3


def from_root(value, axis, source):
    kept = jnp.where(lax.axis_index(axis) == source, value, 0).astype(value.dtype)
    return lax.psum(kept, axis)


def solve_panel(factor, column_tiles, block_ids, panel_index):
    tile_rows, block_size, _ = column_tiles.shape
    stacked = column_tiles.reshape(tile_rows * block_size, block_size)
    solved = jax.scipy.linalg.solve_triangular(factor, stacked.T, lower=True).T
    solved = solved.reshape(tile_rows, block_size, block_size)
    below_mask = (block_ids > panel_index)[:, None, None]
    diag_mask = (block_ids == panel_index)[:, None, None]
    return jnp.where(below_mask, solved, jnp.where(diag_mask, factor[None], jnp.zeros_like(solved)))


def apply_update(matrix, row_panel, col_panel, tile_col, root_col, my_col):
    product = jnp.einsum("trc,sxc->trsx", row_panel, col_panel, precision=lax.Precision.HIGHEST)
    result = matrix - product
    owner_mask = (jnp.arange(matrix.shape[2], dtype=jnp.int32) == tile_col) & (my_col == root_col)
    return jnp.where(owner_mask[None, None, :, None], row_panel[:, :, None, :], result)


def per_device(covariance):
    tile_rows, block_size, tile_cols, _ = covariance.shape
    row_count = lax.axis_size("row")
    col_count = lax.axis_size("col")
    my_row = lax.axis_index("row")
    my_col = lax.axis_index("col")
    row_blocks = jnp.arange(tile_rows, dtype=jnp.int32) * row_count + my_row
    col_blocks = jnp.arange(tile_cols, dtype=jnp.int32) * col_count + my_col
    matrix = covariance
    column_raw = matrix[:, :, 0, :]
    for panel_index in range(PANELS):
        root_row = panel_index % row_count
        tile_row = panel_index // row_count
        root_col = panel_index % col_count
        tile_col = panel_index // col_count
        diagonal = from_root(column_raw[tile_row], "row", root_row)
        factor = jnp.linalg.cholesky(diagonal)
        local_rows = solve_panel(factor, column_raw, row_blocks, panel_index)
        row_panel = from_root(local_rows, "col", root_col)
        pieces = []
        for offset in range(row_count // col_count):
            received = from_root(row_panel, "row", my_col + col_count * offset)
            pieces.append(received)
        col_panel = jnp.stack(pieces, axis=1).reshape(tile_cols, block_size, block_size)
        next_tile = min((panel_index + 1) // col_count, tile_cols - 1)
        matrix = apply_update(matrix, row_panel, col_panel, tile_col, root_col, my_col)
        column_raw = matrix[:, :, next_tile, :]
    within = jnp.arange(block_size, dtype=jnp.int32)
    rows_global = row_blocks[:, None] * block_size + within[None, :]
    cols_global = col_blocks[:, None] * block_size + within[None, :]
    lower_mask = rows_global[:, :, None, None] >= cols_global[None, None, :, :]
    return jnp.where(lower_mask, matrix, jnp.zeros_like(matrix))


def solution(mesh):
    placed = (P(None, "row", None, "col"),)
    return jax.shard_map(
        per_device,
        mesh=mesh,
        in_specs=placed,
        out_specs=P(None, "row", None, "col"),
        check_vma=False,
    )
```

profile of v0, /device:TPU:32, one launch (start us, length us, event | category | flops | bytes accessed | tf_op | source)
XLA Modules:
  0.0 1381.6 jit_solution(6271060636620441325)
XLA Ops:
  6.5 1.2 copy.18
  8.5 159.6 %all-reduce.13.cloned.1.call-done = f32[128,128]{0,1:T(8,128)} async-done(((f32[128,128]{0,1:T(8,128)}), f32[128,128]{0,1:T(8,128)}) %all-reduce.13.cloned.1.call-update) | async-done | bytes 65552 | tf_op jit(solution)/shard_map/psum | solution.py:11
  168.1 1.0 copy.19
  169.1 11.7 cholesky.59
  182.2 9.8 custom-call.7
  192.4 0.7 select_select_fusion.2
  193.2 112.6 %all-reduce.15.cloned.1.call-done = f32[2,128,128]{2,1,0:T(8,128)} async-done(((f32[2,128,128]{2,1,0:T(8,128)}), f32[2,128,128]{2,1,0:T(8,128)}) %all-reduce.15.cloned.1.call-update) | async-done | bytes 131088 | tf_op jit(solution)/shard_map/psum | solution.py:11
  305.8 1.6 select_bitcast_fusion.5
  307.5 0.8 copy-done
  308.4 159.3 %all-reduce.29.cloned.1.call-done = (f32[2,1,128,128]{3,2,0,1:T(8,128)}, f32[2,1,128,128]{3,2,0,1:T(8,128)}) async-done(((f32[2,1,128,128]{3,2,0,1:T(8,128)}, f32[2,1,128,128]{3,2,0,1:T(8,128)}), (f32[2,1,128,128]{3,2,0,1:T(8,128)}, f32[2,1,128,128]{3,2,0,1:T(8,128)})) %all-reduce.29.cloned.1.call-update) | async-done | bytes 262160 | tf_op jit(solution)/shard_map/psum | solution.py:11
  467.7 1.0 pad_maximum_fusion
  470.4 150.3 %all-reduce.17.cloned.1.call-done = f32[128,128]{0,1:T(8,128)} async-done(((f32[128,128]{0,1:T(8,128)}), f32[128,128]{0,1:T(8,128)}) %all-reduce.17.cloned.1.call-update) | async-done | bytes 65552 | tf_op jit(solution)/shard_map/psum | solution.py:11
  620.6 1.0 copy.25
  621.7 11.7 cholesky.70
  634.7 9.8 custom-call.8
  645.0 0.7 select_select_fusion.1
  645.8 112.4 %all-reduce.19.cloned.1.call-done = f32[2,128,128]{2,1,0:T(8,128)} async-done(((f32[2,128,128]{2,1,0:T(8,128)}), f32[2,128,128]{2,1,0:T(8,128)}) %all-reduce.19.cloned.1.call-update) | async-done | bytes 131088 | tf_op jit(solution)/shard_map/psum | solution.py:11
  758.2 1.6 select_bitcast_fusion.3
  759.9 0.7 copy-done.1
  760.8 159.2 %all-reduce.27.cloned.1.call-done = (f32[2,1,128,128]{3,2,0,1:T(8,128)}, f32[2,1,128,128]{3,2,0,1:T(8,128)}) async-done(((f32[2,1,128,128]{3,2,0,1:T(8,128)}, f32[2,1,128,128]{3,2,0,1:T(8,128)}), (f32[2,1,128,128]{3,2,0,1:T(8,128)}, f32[2,1,128,128]{3,2,0,1:T(8,128)})) %all-reduce.27.cloned.1.call-update) | async-done | bytes 262160 | tf_op jit(solution)/shard_map/psum | solution.py:11
  919.9 1.0 pad_maximum_fusion.1
  922.6 150.4 %all-reduce.21.cloned.1.call-done = f32[128,128]{0,1:T(8,128)} async-done(((f32[128,128]{0,1:T(8,128)}), f32[128,128]{0,1:T(8,128)}) %all-reduce.21.cloned.1.call-update) | async-done | bytes 65552 | tf_op jit(solution)/shard_map/psum | solution.py:11
  1073.0 1.0 copy.31
  1074.0 11.7 cholesky.81
  1087.1 9.8 custom-call.9
  1097.3 0.7 select_select_fusion
  1098.1 112.4 %all-reduce.23.cloned.1.call-done = f32[2,128,128]{2,1,0:T(8,128)} async-done(((f32[2,128,128]{2,1,0:T(8,128)}), f32[2,128,128]{2,1,0:T(8,128)}) %all-reduce.23.cloned.1.call-update) | async-done | bytes 131088 | tf_op jit(solution)/shard_map/psum | solution.py:11
  1210.5 1.6 select_bitcast_fusion.1
  1212.2 0.8 copy-done.2
  1213.1 159.3 %all-reduce.25.cloned.1.call-done = (f32[2,1,128,128]{3,2,0,1:T(8,128)}, f32[2,1,128,128]{3,2,0,1:T(8,128)}) async-done(((f32[2,1,128,128]{3,2,0,1:T(8,128)}, f32[2,1,128,128]{3,2,0,1:T(8,128)}), (f32[2,1,128,128]{3,2,0,1:T(8,128)}, f32[2,1,128,128]{3,2,0,1:T(8,128)})) %all-reduce.25.cloned.1.call-update) | async-done | bytes 262160 | tf_op jit(solution)/shard_map/psum | solution.py:11
  1372.5 1.0 pad_maximum_fusion.2
  1374.1 1.0 copy.37
  (73 shorter events, 10.6 us)
Async XLA Ops:
  6.5 161.5 %all-reduce.13.cloned.1.call-start = ((), (), s32[]{:S(2)}) async-start(), calls=%async_computation | async-start | bytes 131072 | tf_op jit(solution)/shard_map/psum | solution.py:11
  8.4 297.4 %all-reduce.15.cloned.1.call-start = ((), (), s32[]{:S(2)}) async-start(), calls=%async_computation.1 | async-start | bytes 262144 | tf_op jit(solution)/shard_map/psum | solution.py:11
  168.1 1.0 copy-start.3
  180.8 11.2 slice-start
  193.2 274.6 %all-reduce.29.cloned.1.call-start = ((), (), s32[]{:S(2)}) async-start(), calls=%async_computation.8 | async-start | bytes 524288 | tf_op jit(solution)/shard_map/psum | solution.py:11
  307.4 0.9 copy-start
  307.4 313.2 %all-reduce.17.cloned.1.call-start = ((), (), s32[]{:S(2)}) async-start(), calls=%async_computation.2 | async-start | bytes 131072 | tf_op jit(solution)/shard_map/psum | solution.py:11
  470.0 288.1 %all-reduce.19.cloned.1.call-start = ((), (), s32[]{:S(2)}) async-start(), calls=%async_computation.3 | async-start | bytes 262144 | tf_op jit(solution)/shard_map/psum | solution.py:11
  620.6 1.0 copy-start.5
  645.7 274.2 %all-reduce.27.cloned.1.call-start = ((), (), s32[]{:S(2)}) async-start(), calls=%async_computation.7 | async-start | bytes 524288 | tf_op jit(solution)/shard_map/psum | solution.py:11
  759.8 0.9 copy-start.1
  759.8 313.2 %all-reduce.21.cloned.1.call-start = ((), (), s32[]{:S(2)}) async-start(), calls=%async_computation.4 | async-start | bytes 131072 | tf_op jit(solution)/shard_map/psum | solution.py:11
  922.2 288.3 %all-reduce.23.cloned.1.call-start = ((), (), s32[]{:S(2)}) async-start(), calls=%async_computation.5 | async-start | bytes 262144 | tf_op jit(solution)/shard_map/psum | solution.py:11
  1073.0 1.0 copy-start.4
  1098.1 274.4 %all-reduce.25.cloned.1.call-start = ((), (), s32[]{:S(2)}) async-start(), calls=%async_computation.6 | async-start | bytes 524288 | tf_op jit(solution)/shard_map/psum | solution.py:11
  1212.1 0.9 copy-start.2
Sparse Core Ops, SparseCore 0:
  10.8 157.2 all-reduce.12
  193.3 112.4 all-reduce.14
  309.3 158.3 all-reduce.28
  471.0 149.5 all-reduce.16
  645.9 112.2 all-reduce.18
  761.5 158.3 all-reduce.26
  923.4 149.5 all-reduce.20
  1098.2 112.2 all-reduce.22
  1214.0 158.3 all-reduce.24
where the time goes:
time: 1380 us
  waiting for transfers between devices  1280 us (93%)
  other arithmetic  80.7 us (6%)
    psum x9, waiting for transfers between devices, from_root(): return lax.psum(kept, axis)  1280 us
    another operation x9, other arithmetic, per_device(): factor = jnp.linalg.cholesky(diagonal)  37.2 us
    another operation x6, other arithmetic, solve_panel(): solved = jax.scipy.linalg.solve_triangular(factor, stacked.T, lower=True).T  31.4 us
  transfers between devices with their start and end apart: 9, of which 9 were waited for; matrix products, arithmetic and copies ran while one was open for 0% of the time, Pallas kernels for 0%

commit v1 on v0

v1 whole, which is shorter than its diff:
```python
import jax
import jax.numpy as jnp
from jax import lax
from jax.sharding import PartitionSpec as P

PANELS = 3
UPPER = [(i, j) for i in range(PANELS) for j in range(i, PANELS)]


def mm(a, b):
    return jnp.dot(a, b, precision=lax.Precision.HIGHEST, preferred_element_type=jnp.float32)


def gather_leading_rows(matrix, row_count, col_count):
    tile_rows, nb, tile_cols, _ = matrix.shape
    part = nb // row_count
    split = matrix[0].reshape(row_count, part, tile_cols, nb).transpose(0, 2, 1, 3)
    piece = lax.all_to_all(split, "row", 0, 0)[:PANELS]
    everyone = lax.all_gather(piece, "col")
    groups = row_count // col_count
    by_row = everyone.reshape(col_count, PANELS, tile_rows, groups, part, nb)
    by_row = by_row.transpose(3, 0, 1, 2, 4, 5).reshape(row_count, PANELS * tile_rows, part, nb)
    lead = jnp.stack([everyone[j, i, 0] for i, j in UPPER])
    lead = jnp.broadcast_to(lead[None], (row_count,) + lead.shape)
    mine = piece.reshape(1, PANELS * tile_cols, part, nb)
    mine = jnp.broadcast_to(mine, (row_count,) + mine.shape[1:])
    packed = jnp.concatenate([mine, by_row, lead], axis=1)
    count = packed.shape[1]
    packed = packed.reshape(row_count, count * part, nb)
    got = lax.all_to_all(packed, "row", 0, 0)
    tiles = got.reshape(row_count, count, part, nb).transpose(1, 0, 2, 3).reshape(count, nb, nb)
    y_tiles = tiles[: PANELS * tile_cols].reshape(PANELS, tile_cols, nb, nb)
    x_tiles = tiles[PANELS * tile_cols : PANELS * (tile_cols + tile_rows)].reshape(PANELS, tile_rows, nb, nb)
    lead_tiles = tiles[PANELS * (tile_cols + tile_rows) :]
    return lead_tiles, x_tiles, y_tiles


def per_device(matrix):
    tile_rows, nb, tile_cols, _ = matrix.shape
    row_count = lax.axis_size("row")
    col_count = lax.axis_size("col")
    my_row = lax.axis_index("row")
    my_col = lax.axis_index("col")
    lead_tiles, x_tiles, y_tiles = gather_leading_rows(matrix, row_count, col_count)
    lead = dict(zip(UPPER, [lead_tiles[n] for n in range(len(UPPER))]))
    rest = [
        jnp.concatenate([x_tiles[i, t] for t in range(tile_rows)] + [y_tiles[i, s] for s in range(tile_cols)], axis=1)
        for i in range(PANELS)
    ]
    eye = jnp.eye(nb, dtype=jnp.float32)
    solved = []
    for k in range(PANELS):
        factor = jnp.linalg.cholesky(lead[k, k])
        inverse = jax.scipy.linalg.solve_triangular(factor, eye, lower=True)
        wide = jnp.concatenate([lead[k, j] for j in range(k + 1, PANELS)] + [rest[k]], axis=1)
        wide = mm(inverse, wide)
        skip = (PANELS - 1 - k) * nb
        solved.append(wide[:, skip:])
        for i in range(k + 1, PANELS):
            left = wide[:, (i - k - 1) * nb : (i - k) * nb].T
            change = mm(left, wide[:, (i - k - 1) * nb :])
            for j in range(i, PANELS):
                lead[i, j] = lead[i, j] - change[:, (j - i) * nb : (j - i + 1) * nb]
            rest[i] = rest[i] - change[:, (PANELS - i) * nb :]
    upper = jnp.concatenate(solved, axis=0)
    rows_t = upper[:, : tile_rows * nb]
    cols = upper[:, tile_rows * nb :]
    product = lax.dot_general(rows_t, cols, (((0,), (0,)), ((), ())), precision=lax.Precision.HIGHEST)
    result = matrix - product.reshape(tile_rows, nb, tile_cols, nb)
    panel = jnp.stack([s[:, : tile_rows * nb] for s in solved])
    panel = lax.dynamic_index_in_dim(panel, jnp.minimum(my_col, PANELS - 1), 0, keepdims=False).T
    panel = panel.reshape(tile_rows, nb, nb)
    owner = (jnp.arange(tile_cols) == 0) & (my_col < PANELS)
    result = jnp.where(owner[None, None, :, None], panel[:, :, None, :], result)
    row_blocks = jnp.arange(tile_rows, dtype=jnp.int32) * row_count + my_row
    col_blocks = jnp.arange(tile_cols, dtype=jnp.int32) * col_count + my_col
    within = jnp.arange(nb, dtype=jnp.int32)
    rows_global = row_blocks[:, None] * nb + within[None, :]
    cols_global = col_blocks[:, None] * nb + within[None, :]
    lower_mask = rows_global[:, :, None, None] >= cols_global[None, None, :, :]
    return jnp.where(lower_mask, result, jnp.zeros_like(result))


def solution(mesh):
    placed = (P(None, "row", None, "col"),)
    return jax.shard_map(
        per_device,
        mesh=mesh,
        in_specs=placed,
        out_specs=P(None, "row", None, "col"),
        check_vma=False,
    )
```

time: 1380 us -> 171 us (0.12)
  the two profiles are of different devices: /device:TPU:32 before, /device:TPU:5 now
where the time goes in v1:
time: 171 us
  other arithmetic  72 us (42%)
  blocking collectives  43.6 us (25%)
  waiting for transfers between devices  39.1 us (23%)
  matrix products  5.26 us (3%)
  starting transfers between devices  5.18 us (3%)
  local copies, waits for them, and re-layouts  4.89 us (3%)
    all_to_all x1, waiting for transfers between devices, gather_leading_rows(): got = lax.all_to_all(packed, 'row', 0, 0)  39.1 us
    another operation x9, other arithmetic, per_device(): factor = jnp.linalg.cholesky(lead[k, k])  37.5 us
    another operation x6, other arithmetic, per_device(): inverse = jax.scipy.linalg.solve_triangular(factor, eye, lower=True)  31.5 us
    all_to_all x1, blocking collectives, gather_leading_rows(): piece = lax.all_to_all(split, 'row', 0, 0)[:PANELS]  23.1 us
    all_gather x1, blocking collectives, gather_leading_rows(): everyone = lax.all_gather(piece, 'col')  20.5 us
    all_to_all x1, starting transfers between devices, gather_leading_rows(): got = lax.all_to_all(packed, 'row', 0, 0)  5.18 us
  transfers between devices with their start and end apart: 1, of which 1 were waited for; matrix products, arithmetic and copies ran while one was open for 0% of the time, Pallas kernels for 0%

profile of v1, /device:TPU:5, one launch (start us, length us, event | category | flops | bytes accessed | tf_op | source)
XLA Modules:
  0.0 170.6 jit_solution(3306241417307610977)
XLA Ops:
  0.0 1.0 slice.182
  1.1 23.1 %all_to_all.10 = f32[32,4,4,128]{3,2,1,0:T(4,128)S(1)} all-to-all(f32[32,4,4,128]{3,2,1,0:T(4,128)S(1)} %copy.98), channel_id=1, replica_groups=mesh['row'=32,'col'=16] {'row'}, dimensions={0} | all-to-all | bytes 524288 | tf_op jit(solution)/shard_map/all_to_all | solution.py:18
  24.1 20.5 %all-gather = f32[48,4,4,128]{3,2,1,0:T(4,128)S(1)} all-gather(f32[3,4,4,128]{3,2,1,0:T(4,128)S(1)} %slice.234), channel_id=2, replica_groups=mesh['row'=32,'col'=16] {'col'}, dimensions={0}, use_global_device_ids=true | all-gather | bytes 417792 | tf_op jit(solution)/shard_map/all_gather | solution.py:19
  45.3 1.6 pad_maximum_fusion
  46.9 5.2 %all-to-all-start.1 = ((f32[32,96,128]{2,1,0:T(8,128)}), f32[32,96,128]{2,1,0:T(8,128)S(1)}, u32[]{:S(2)}, u32[]{:S(2)}) async-start(f32[32,96,128]{2,1,0:T(8,128)} %bitcast.13), calls=%async_computation.1 | async-start | bytes 3145728 | tf_op jit(solution)/shard_map/all_to_all | solution.py:30
  52.2 39.1 %all-to-all-done.1 = f32[32,96,128]{2,1,0:T(8,128)S(1)} async-done(((f32[32,96,128]{2,1,0:T(8,128)}), f32[32,96,128]{2,1,0:T(8,128)S(1)}, u32[]{:S(2)}, u32[]{:S(2)}) %all-to-all-start.1) | async-done | bytes 1572896 | tf_op jit(solution)/shard_map/all_to_all | solution.py:30
  91.3 0.9 copy.101
  92.4 0.3 copy.106
  92.6 0.5 copy.107
  93.4 11.7 %cholesky.59 = f32[128,128]{1,0:T(8,128)S(1)} custom-call(f32[128,128]{1,0:T(8,128)S(1)} %fusion.54), custom_call_target="Cholesky" | custom-call | tf_op jit(solution)/shard_map/jit(cholesky)/cholesky | solution.py:53
  105.2 0.6 compare_reduce_fusion.2
  105.8 0.7 fusion.23
  106.5 9.8 %custom-call.7 = f32[1,128,128]{1,2,0:T(8,128)S(1)} custom-call(f32[1,128,128]{2,1,0:T(8,128)S(1)} %fusion.23), custom_call_target="InvertDiagBlocksLowerTriangular" | custom-call | tf_op jit(solution)/shard_map/jit(_solve_triangular)/triangular_solve | solution.py:54
  116.3 0.3 fusion.21
  116.8 0.6 fusion.58
  117.4 0.6 fusion.2
  118.0 0.6 fusion.41
  119.1 11.8 %cholesky.70 = f32[128,128]{1,0:T(8,128)S(1)} custom-call(f32[128,128]{1,0:T(8,128)S(1)} %fusion.52), custom_call_target="Cholesky" | custom-call | tf_op jit(solution)/shard_map/jit(cholesky)/cholesky | solution.py:53
  131.0 0.7 compare_reduce_fusion.1
  131.7 0.7 fusion.24
  132.4 9.8 %custom-call.8 = f32[1,128,128]{1,2,0:T(8,128)S(1)} custom-call(f32[1,128,128]{2,1,0:T(8,128)S(1)} %fusion.24), custom_call_target="InvertDiagBlocksLowerTriangular" | custom-call | tf_op jit(solution)/shard_map/jit(_solve_triangular)/triangular_solve | solution.py:54
  142.3 0.3 fusion.19
  142.5 0.5 fusion.4
  143.1 0.6 fusion.32
  144.2 11.7 %cholesky.81 = f32[128,128]{1,0:T(8,128)S(1)} custom-call(f32[128,128]{1,0:T(8,128)S(1)} %fusion.50), custom_call_target="Cholesky" | custom-call | tf_op jit(solution)/shard_map/jit(cholesky)/cholesky | solution.py:53
  155.9 0.7 compare_reduce_fusion
  156.7 0.7 fusion.25
  157.4 9.8 %custom-call.9 = f32[1,128,128]{1,2,0:T(8,128)S(1)} custom-call(f32[1,128,128]{2,1,0:T(8,128)S(1)} %fusion.25), custom_call_target="InvertDiagBlocksLowerTriangular" | custom-call | tf_op jit(solution)/shard_map/jit(_solve_triangular)/triangular_solve | solution.py:54
  167.2 0.3 fusion.17
  167.5 0.5 fusion.13
  168.2 1.0 fusion
  169.4 1.1 select_select_fusion
  (67 shorter events, 2.7 us)
Async XLA Ops:
  46.9 44.4 %all-to-all-start.1 = ((f32[32,96,128]{2,1,0:T(8,128)}), f32[32,96,128]{2,1,0:T(8,128)S(1)}, u32[]{:S(2)}, u32[]{:S(2)}) async-start(f32[32,96,128]{2,1,0:T(8,128)} %bitcast.13), calls=%async_computation.1 | async-start | bytes 3145728 | tf_op jit(solution)/shard_map/all_to_all | solution.py:30
  117.4 1.2 copy-start
  157.4 10.8 %slice-start = ((f32[128,1024]{1,0:T(8,128)}), f32[128,768]{1,0:T(8,128)S(1)}, s32[]{:S(2)}) async-start(f32[128,1024]{1,0:T(8,128)} %copy-done), calls=%async_computation.2 | async-start | bytes 786432 | tf_op jit(solution)/shard_map/slice | solution.py:58
  168.2 1.3 copy-start.1

commit v2 on v0

v2 whole, which is shorter than its diff:
```python
import jax
import jax.numpy as jnp
from jax import lax
from jax.experimental import pallas as pl
from jax.experimental.pallas import tpu as pltpu
from jax.sharding import PartitionSpec as P


NB = 128
PANELS = 3
STRIP = 16
NX = 4
NZ = 8
PART = NB // NZ
UPPER = [(i, j) for i in range(PANELS) for j in range(i, PANELS)]
VMEM = pl.BlockSpec(memory_space=pltpu.VMEM)
SMEM = pl.BlockSpec(memory_space=pltpu.SMEM)


def mm(a, b):
    return jnp.dot(a, b, precision=lax.Precision.HIGHEST, preferred_element_type=jnp.float32)


def factor_strip(strip, first):
    n = strip.shape[0]
    rows = lax.broadcasted_iota(jnp.int32, (n, NB), 0)
    cols = [jnp.broadcast_to(strip[:, first + i : first + i + 1], (n, NB)) for i in range(n)]
    parts = [strip[:, q * NB : (q + 1) * NB] for q in range(strip.shape[1] // NB)]
    upper = list(parts)
    pivots = jnp.ones((n, NB), jnp.float32)
    for i in range(n):
        here = rows == i
        pivot = jnp.broadcast_to(cols[i][i : i + 1, :], (n, NB))
        scale = 1.0 / pivot
        pivots = jnp.where(here, pivot, pivots)
        lift = jnp.where(here, 0.0, cols[i] * scale)
        for j in range(i + 1, n):
            cols[j] = cols[j] - lift * jnp.broadcast_to(cols[j][i : i + 1, :], (n, NB))
        upper = [jnp.where(here, p, u) for p, u in zip(parts, upper)]
        parts = [p - lift * jnp.broadcast_to(p[i : i + 1, :], (n, NB)) for p in parts]
    root = lax.rsqrt(pivots)
    inverse = 1.0 / pivots
    upper = jnp.concatenate([u * root for u in upper], axis=1)
    solved = jnp.concatenate([p * inverse for p in parts], axis=1)
    return upper, solved


def factor_kernel(lead_ref, inv_ref, low_ref, work, upper):
    eye = lax.broadcasted_iota(jnp.int32, (NB, NB), 0) == lax.broadcasted_iota(jnp.int32, (NB, NB), 1)
    eye = eye.astype(jnp.float32)
    zero = jnp.zeros((NB, NB), jnp.float32)
    for k in range(PANELS):
        for q, j in zip((0, 2, 3), (k, k + 1, k + 2)):
            tile = lead_ref[:, UPPER.index((k, j)) * PART :, :][:, :PART, :].reshape(NB, NB) if j < PANELS else zero
            work[k, :, q * NB : (q + 1) * NB] = tile
        work[k, :, NB : 2 * NB] = eye

    def panel(k, carry):
        strip = work[k, 0:STRIP, :]
        for b in range(NB // STRIP):
            first = b * STRIP
            rows_u, solved = factor_strip(strip, first)
            upper[first : first + STRIP, :] = rows_u
            rest = NB - first - STRIP
            if rest:
                pieces = [jnp.zeros((first, 4 * NB), jnp.float32)] if first else []
                pieces += [solved, jnp.zeros((rest, 4 * NB), jnp.float32)]
                padded = jnp.concatenate(pieces, axis=0)
                below = work[k, first + STRIP :, :]
                below = below - mm(below[:, :NB], padded)
                strip = below[:STRIP]
                if rest > STRIP:
                    work[k, first + 2 * STRIP :, :] = below[STRIP:]
        inv_ref[k] = upper[:, NB : 2 * NB]

        @pl.when(k < PANELS - 1)
        def _():
            u1 = upper[:, 2 * NB : 3 * NB]
            u2 = upper[:, 3 * NB :]
            l1 = u1.T
            l2 = u2.T
            low_ref[k, 0] = l1
            low_ref[k, 1] = l2
            work[k + 1, :, :NB] -= mm(l1, u1)
            work[k + 1, :, 2 * NB : 3 * NB] -= mm(l1, u2)
            work[k + 2, :, :NB] -= mm(l2, u2)

        return carry

    lax.fori_loop(0, PANELS, panel, 0)


def factor(lead):
    return pl.pallas_call(
        factor_kernel,
        out_shape=(
            jax.ShapeDtypeStruct((PANELS, NB, NB), jnp.float32),
            jax.ShapeDtypeStruct((PANELS - 1, 2, NB, NB), jnp.float32),
        ),
        in_specs=[VMEM],
        out_specs=[VMEM, VMEM],
        scratch_shapes=[
            pltpu.VMEM((PANELS + 1, NB, 4 * NB), jnp.float32),
            pltpu.VMEM((NB, 4 * NB), jnp.float32),
        ],
        name="factor",
    )(lead)


def mm_nt(a, b):
    return lax.dot_general(
        a, b, (((1,), (1,)), ((), ())), precision=lax.Precision.HIGHEST, preferred_element_type=jnp.float32
    )


def pack_kernel(place_ref, own_ref, one_ref, two_ref, three_ref, out_ref, got):
    for d, ref in enumerate((own_ref, one_ref, two_ref, three_ref)):
        got[d] = ref[...]
    my_x = lax.rem(place_ref[0], NX)
    for p, (i, j) in enumerate(UPPER):
        tile = got[lax.rem(my_x + NX - i, NX), j * PART : (j + 1) * PART, :]
        for z in range(NZ):
            out_ref[z, p * PART : (p + 1) * PART, :] = tile


def pack(place, pieces):
    shape = pieces[0].shape
    return pl.pallas_call(
        pack_kernel,
        out_shape=jax.ShapeDtypeStruct((NZ, len(UPPER) * PART, NB), jnp.float32),
        in_specs=[SMEM] + [VMEM] * len(pieces),
        out_specs=VMEM,
        scratch_shapes=[pltpu.VMEM((len(pieces),) + shape, jnp.float32)],
        name="pack",
    )(place, *pieces)


def finish_kernel(place_ref, inv_ref, low_ref, x_ref, y_ref, m_ref, out_ref):
    my_row = place_ref[0]
    my_col = place_ref[1]
    col_count = place_ref[2]
    row_count = NX * NZ
    odd = lax.rem(my_col // 2, 2)
    left = [x_ref[0, odd], x_ref[1, odd], x_ref[0, 1 - odd]]
    rows0 = mm_nt(left[0], inv_ref[0])
    rows1 = mm_nt(left[1] - mm_nt(rows0, low_ref[0, 0]), inv_ref[1])
    rows2 = mm_nt(left[2] - mm_nt(rows0, low_ref[0, 1]) - mm_nt(rows1, low_ref[1, 0]), inv_ref[2])
    right = []
    for i in range(PANELS):
        right.append(jnp.concatenate([y_ref[i, pl.ds(s, NB, stride=4), :] for s in range(4)], axis=1))
    cols0 = mm(inv_ref[0], right[0])
    cols1 = mm(inv_ref[1], right[1] - mm(low_ref[0, 0], cols0))
    cols2 = mm(inv_ref[2], right[2] - mm(low_ref[0, 1], cols0) - mm(low_ref[1, 0], cols1))
    rows = jnp.concatenate([rows0, rows1, rows2], axis=1)
    product = mm(rows, jnp.concatenate([cols0, cols1, cols2], axis=0))
    panel = jnp.where(my_col == 0, rows0, jnp.where(my_col == 1, rows1, rows2))
    u = lax.broadcasted_iota(jnp.int32, (NB, NB), 0)
    v = lax.broadcasted_iota(jnp.int32, (NB, NB), 1)
    for t in range(2):
        for s in range(4):
            value = m_ref[t, pl.ds(s, NB, stride=4), :] - product[t * NB : (t + 1) * NB, s * NB : (s + 1) * NB]
            if s == 0:
                value = jnp.where(my_col < PANELS, panel[t * NB : (t + 1) * NB], value)
            below = (t * row_count + my_row - s * col_count - my_col) * NB
            out_ref[t, pl.ds(s, NB, stride=4), :] = jnp.where(below + u >= v, value, 0.0)


def finish(place, inverse, low, x_part, y_part, matrix):
    return pl.pallas_call(
        finish_kernel,
        out_shape=jax.ShapeDtypeStruct(matrix.shape, jnp.float32),
        in_specs=[SMEM] + [VMEM] * 5,
        out_specs=VMEM,
        name="finish",
    )(place, inverse, low, x_part, y_part, matrix)


def to_all(value, axis, groups):
    count = len(groups[0])
    return lax.all_to_all(jnp.broadcast_to(value[None], (count,) + value.shape), axis, 0, 0, axis_index_groups=groups)


def per_device(covariance):
    tile_rows, nb, tile_cols, _ = covariance.shape
    col_count = lax.axis_size("col")
    my_col = lax.axis_index("col")
    place = jnp.stack([lax.axis_index("row"), my_col, jnp.int32(col_count)])
    matrix = covariance.reshape(tile_rows, nb * tile_cols, nb)
    along_z = [[z * NX + x for z in range(NZ)] for x in range(NX)]
    along_y = [[c for c in range(q, col_count, 2)] for q in range(2)]
    pairs = [[c, c + 1] for c in range(0, col_count, 2)]
    half, quarter = col_count // 2, col_count // 4

    mine = covariance[:, :, 0, :].reshape(tile_rows * nb, nb)
    far = lax.ppermute(mine, "col", [(c, c + half) for c in range(PANELS)])
    mine = jnp.where(my_col >= half, far, mine)
    mid = lax.ppermute(mine, "col", [(c + h, c + h + quarter) for c in range(PANELS) for h in (0, half)])
    mine = jnp.where(my_col % half >= quarter, mid, mine)
    steps = []
    for start in range(0, col_count, quarter):
        steps += [(start, start + 2), (start + 1, start + 3), (start + 2, start)]
    near = lax.ppermute(mine, "col", steps)
    x_part = lax.all_gather(jnp.stack([mine, near]), "col", axis_index_groups=pairs)

    piece = lax.all_to_all(matrix[0].reshape(NZ, PART * tile_cols, nb), "row", 0, 0, axis_index_groups=along_z)[0]
    y_block = to_all(piece, "row", along_z).reshape(nb * tile_cols, nb)
    head = piece.reshape(PART, tile_cols, nb)[:, 0, :]
    own = to_all(head, "col", along_y)[:2]
    both = lax.all_gather(own, "col", axis_index_groups=pairs)
    lead = jnp.concatenate([both[j % 2, j // 2] for j in range(PANELS)], axis=0)
    pieces = [lead]
    for d in range(1, NX):
        hops = [(z * NX + x, z * NX + (x + d) % NX) for z in range(NZ) for x in range(PANELS)]
        pieces.append(lax.ppermute(lead, "row", hops))
    lead = pack(place, pieces)
    lead = lax.all_to_all(lead, "row", 0, 0, axis_index_groups=along_z)
    along_x = [[z * NX + x for x in range(NX)] for z in range(NZ)]
    y_part = to_all(y_block, "row", along_x)
    inverse, low = factor(lead)
    out = finish(place, inverse, low, x_part, y_part, matrix)
    return out.reshape(covariance.shape)


def solution(mesh):
    placed = (P(None, "row", None, "col"),)
    return jax.shard_map(
        per_device,
        mesh=mesh,
        in_specs=placed,
        out_specs=P(None, "row", None, "col"),
        check_vma=False,
    )
```

time: 1380 us -> 124 us (0.09)
  the two profiles are of different devices: /device:TPU:32 before, /device:TPU:27 now
where the time goes in v2:
time: 124 us
  blocking collectives  35 us (28%)
  starting transfers between devices  33.3 us (27%)
  waiting for transfers between devices  26.7 us (22%)
  Pallas kernels  22.2 us (18%)
  local copies, waits for them, and re-layouts  5.5 us (4%)
    all_to_all x1, blocking collectives, per_device(): lax.all_to_all(matrix[0].reshape(NZ, PART * tile_cols, nb), 'row', 0, 0,...  20.3 us
    all_to_all x3, starting transfers between devices, to_all(): lax.all_to_all(jnp.broadcast_to(value[None], (count,) + value.shape), axi...  14.2 us
    pallas_call x1, Pallas kernels, factor(): pl.pallas_call(factor_kernel, out_shape=(jax.ShapeDtypeStruct((PANELS, NB...  14.2 us
    all_to_all x1, waiting for transfers between devices, per_device(): lead = lax.all_to_all(lead, 'row', 0, 0, axis_index_groups=along_z)  11.8 us
    ppermute x1, waiting for transfers between devices, per_device(): near = lax.ppermute(mine, 'col', steps)  10.6 us
    ppermute x3, starting transfers between devices, per_device(): pieces.append(lax.ppermute(lead, 'row', hops))  9.63 us
    all_gather x1, blocking collectives, per_device(): lax.all_gather(jnp.stack([mine, near]), 'col', axis_index_groups=pairs)  9.43 us
    all_to_all x1, starting transfers between devices, per_device(): lead = lax.all_to_all(lead, 'row', 0, 0, axis_index_groups=along_z)  6.82 us
  transfers between devices with their start and end apart: 10, of which 4 were waited for; matrix products, arithmetic and copies ran while one was open for 2% of the time, Pallas kernels for 13%

profile of v2, /device:TPU:27, one launch (start us, length us, event | category | flops | bytes accessed | tf_op | source)
XLA Modules:
  0.0 123.5 jit_solution(480607697182582612)
XLA Ops:
  0.0 0.9 slice-done
  1.0 20.3 %all_to_all.25 = f32[8,64,128]{2,1,0:T(8,128)S(1)} all-to-all(f32[8,64,128]{2,1,0:T(8,128)S(1)} %bitcast.23), channel_id=1, replica_groups={{0,64,128,192,256,320,384,448},{16,80,144,208,272,336,400,464},{32,96,1..., dimensions={0} | all-to-all | bytes 524288 | tf_op jit(solution)/shard_map/all_to_all | solution.py:205
  21.3 0.6 broadcast_in_dim.22
  21.9 6.8 %all-to-all-start.1 = ((f32[8,16,128]{2,1,0:T(8,128)}), f32[8,16,128]{2,1,0:T(8,128)S(1)}, u32[]{:S(2)}, u32[]{:S(2)}) async-start(f32[8,16,128]{2,1,0:T(8,128)} %broadcast_in_dim.22), calls=%async_computation.1 | async-start | bytes 131072 | tf_op jit(solution)/shard_map/all_to_all | solution.py:180
  28.7 4.1 %all-to-all-done.1 = f32[8,16,128]{2,1,0:T(8,128)S(1)} async-done(((f32[8,16,128]{2,1,0:T(8,128)}), f32[8,16,128]{2,1,0:T(8,128)S(1)}, u32[]{:S(2)}, u32[]{:S(2)}) %all-to-all-start.1) | async-done | bytes 65568 | tf_op jit(solution)/shard_map/all_to_all | solution.py:180
  32.8 0.7 broadcast_in_dim.24
  33.5 3.4 %all-to-all-start.3 = ((f32[8,64,128]{2,1,0:T(8,128)}), f32[8,64,128]{2,1,0:T(8,128)S(1)}, u32[]{:S(2)}, u32[]{:S(2)}) async-start(f32[8,64,128]{2,1,0:T(8,128)} %broadcast_in_dim.24), calls=%async_computation.3 | async-start | bytes 524288 | tf_op jit(solution)/shard_map/all_to_all | solution.py:180
  36.9 5.2 %all-gather = f32[4,16,128]{2,1,0:T(8,128)S(1)} all-gather(f32[2,16,128]{2,1,0:T(8,128)S(1)} %slice.35), channel_id=2, replica_groups={{0,1},{2,3},{4,5},{6,7},{8,9},{10,11},{12,13},{14,15},{16,17},{18,19},{..., dimensions={0}, use_global_device_ids=true | all-gather | bytes 49152 | tf_op jit(solution)/shard_map/all_gather | solution.py:209
  42.2 2.2 %collective-permute-start.2 = (f32[48,128]{1,0:T(8,128)S(1)}, f32[48,128]{1,0:T(8,128)S(1)}, u32[]{:S(2)}, u32[]{:S(2)}) collective-permute-start(f32[48,128]{1,0:T(8,128)S(1)} %pad_maximum_fusion.1.own_ref), channel_id=1, source_target_pairs={{0,48},{16,0},{32,16},{64,112},{80,64},{96,80},{128,176},{144,128}... | collective-permute-start | bytes 73736 | tf_op jit(solution)/shard_map/ppermute | solution.py:214
  44.4 2.9 %collective-permute-start.1 = (f32[48,128]{1,0:T(8,128)S(1)}, f32[48,128]{1,0:T(8,128)S(1)}, u32[]{:S(2)}, u32[]{:S(2)}) collective-permute-start(f32[48,128]{1,0:T(8,128)S(1)} %pad_maximum_fusion.1.own_ref), channel_id=1, source_target_pairs={{0,32},{16,48},{32,0},{64,96},{80,112},{96,64},{128,160},{144,176}... | collective-permute-start | bytes 73736 | tf_op jit(solution)/shard_map/ppermute | solution.py:214
  47.2 4.6 %collective-permute-start = (f32[48,128]{1,0:T(8,128)S(1)}, f32[48,128]{1,0:T(8,128)S(1)}, u32[]{:S(2)}, u32[]{:S(2)}) collective-permute-start(f32[48,128]{1,0:T(8,128)S(1)} %pad_maximum_fusion.1.own_ref), channel_id=1, source_target_pairs={{0,16},{16,32},{32,48},{64,80},{80,96},{96,112},{128,144},{144,160... | collective-permute-start | bytes 73736 | tf_op jit(solution)/shard_map/ppermute | solution.py:214
  51.9 0.7 pad_add_fusion.place_ref
  52.5 0.0 collective-permute-done.1.two_ref
  52.5 0.2 collective-permute-done.one_ref
  52.8 0.3 copy-done.4
  53.1 0.0 copy-done.5
  53.1 0.6 copy-done.6
  53.7 1.6 %pack.1 = f32[8,96,128]{2,1,0:T(8,128)} custom-call(s32[3]{0:T(128)} %pad_add_fusion.place_ref, f32[48,128]{1,0:T(8,128)} %copy-done.3, f32[48,128]{1,0:T(8,128)} %copy-done.6, f32[48,128]{1,0:T(8,128)} %copy-done.5, f32[48,128]{1,0:T(8,128)} %copy-done.4), custom_call_target="tpu_custom_call" | custom-call | tf_op jit(solution)/shard_map/pack/pallas_call | solution.py:128
  55.3 0.0 all-to-all-done.3
  55.3 6.8 %all-to-all-start.2 = ((f32[8,96,128]{2,1,0:T(8,128)}), f32[8,96,128]{2,1,0:T(8,128)S(1)}, u32[]{:S(2)}, u32[]{:S(2)}) async-start(f32[8,96,128]{2,1,0:T(8,128)} %pack.1), calls=%async_computation.2 | async-start | bytes 786432 | tf_op jit(solution)/shard_map/all_to_all | solution.py:216
  62.1 0.1 slice.32
  62.2 0.7 collective-permute-start.3
  62.9 11.8 %all-to-all-done.2.lead_ref = f32[8,96,128]{2,1,0:T(8,128)S(1)} async-done(((f32[8,96,128]{2,1,0:T(8,128)}), f32[8,96,128]{2,1,0:T(8,128)S(1)}, u32[]{:S(2)}, u32[]{:S(2)}) %all-to-all-start.2) | async-done | bytes 393248 | tf_op jit(solution)/shard_map/all_to_all | solution.py:216
  74.7 1.1 broadcast_in_dim.26
  75.8 4.0 %all-to-all-start.4 = ((f32[4,512,128]{2,1,0:T(8,128)}), f32[4,512,128]{2,1,0:T(8,128)S(1)}, u32[]{:S(2)}, u32[]{:S(2)}) async-start(f32[4,512,128]{2,1,0:T(8,128)} %broadcast_in_dim.26), calls=%async_computation.4 | async-start | bytes 2097152 | tf_op jit(solution)/shard_map/all_to_all | solution.py:180
  79.9 0.7 collective-permute-start.4
  80.6 1.3 %collective-permute-start.5 = (f32[256,128]{1,0:T(8,128)S(1)}, f32[256,128]{1,0:T(8,128)S(1)}, u32[]{:S(2)}, u32[]{:S(2)}) collective-permute-start(f32[256,128]{1,0:T(8,128)S(1)} %broadcast_select_fusion.1), channel_id=1, source_target_pairs={{0,2},{1,3},{2,0},{4,6},{5,7},{6,4},{8,10},{9,11},{10,8},{12,14},{... | collective-permute-start | bytes 393224 | tf_op jit(solution)/shard_map/ppermute | solution.py:202
  81.9 10.6 %collective-permute-done.5 = f32[256,128]{1,0:T(8,128)S(1)} collective-permute-done((f32[256,128]{1,0:T(8,128)S(1)}, f32[256,128]{1,0:T(8,128)S(1)}, u32[]{:S(2)}, u32[]{:S(2)}) %collective-permute-start.5) | collective-permute-done | bytes 131104 | tf_op jit(solution)/shard_map/ppermute | solution.py:202
  92.5 9.4 %all-gather.1 = f32[4,256,128]{2,1,0:T(8,128)} all-gather(f32[2,256,128]{2,1,0:T(8,128)S(1)} %pad_maximum_fusion), channel_id=3, replica_groups={{0,1},{2,3},{4,5},{6,7},{8,9},{10,11},{12,13},{14,15},{16,17},{18,19},{..., dimensions={0}, use_global_device_ids=true | all-gather | bytes 786432 | tf_op jit(solution)/shard_map/all_gather | solution.py:203
  101.9 14.2 %factor.1 = (f32[3,128,128]{2,1,0:T(8,128)}, f32[2,2,128,128]{3,2,1,0:T(8,128)}) custom-call(f32[8,96,128]{2,1,0:T(8,128)} %copy-done.2), custom_call_target="tpu_custom_call" | custom-call | tf_op jit(solution)/shard_map/factor/pallas_call | solution.py:94
  116.1 1.0 copy-done
  117.1 6.4 %finish.1 = f32[2,512,128]{2,1,0:T(8,128)} custom-call(s32[3]{0:T(128)} %pad_add_fusion.place_ref, f32[3,128,128]{2,1,0:T(8,128)} %get-tuple-element.7.inv_ref, f32[2,2,128,128]{3,2,1,0:T(8,128)} %get-tuple-element.8.low_ref, f32[2,2,256,128]{3,2,1,0:T(8,128)} %bitcast.21, f32[4,512,128]{2,1,0:T(8,128)} %copy-done, f32[2,512,128]{2,1,0:T(8,128)} %bitcast.22), custom_call_target="tpu_custom_call" | custom-call | tf_op jit(solution)/shard_map/finish/pallas_call | solution.py:169
  (23 shorter events, 0.1 us)
Async XLA Ops:
  0.0 0.9 slice-start
  21.9 10.9 %all-to-all-start.1 = ((f32[8,16,128]{2,1,0:T(8,128)}), f32[8,16,128]{2,1,0:T(8,128)S(1)}, u32[]{:S(2)}, u32[]{:S(2)}) async-start(f32[8,16,128]{2,1,0:T(8,128)} %broadcast_in_dim.22), calls=%async_computation.1 | async-start | bytes 131072 | tf_op jit(solution)/shard_map/all_to_all | solution.py:180
  33.5 21.8 %all-to-all-start.3 = ((f32[8,64,128]{2,1,0:T(8,128)}), f32[8,64,128]{2,1,0:T(8,128)S(1)}, u32[]{:S(2)}, u32[]{:S(2)}) async-start(f32[8,64,128]{2,1,0:T(8,128)} %broadcast_in_dim.24), calls=%async_computation.3 | async-start | bytes 524288 | tf_op jit(solution)/shard_map/all_to_all | solution.py:180
  42.2 10.6 %copy-start.3 = (f32[48,128]{1,0:T(8,128)}, f32[48,128]{1,0:T(8,128)S(1)}, u32[]{:S(2)}) copy-start(f32[48,128]{1,0:T(8,128)S(1)} %pad_maximum_fusion.1.own_ref) | copy-start | bytes 73732
  42.2 10.3 %collective-permute-start.2 = (f32[48,128]{1,0:T(8,128)S(1)}, f32[48,128]{1,0:T(8,128)S(1)}, u32[]{:S(2)}, u32[]{:S(2)}) collective-permute-start(f32[48,128]{1,0:T(8,128)S(1)} %pad_maximum_fusion.1.own_ref), channel_id=1, source_target_pairs={{0,48},{16,0},{32,16},{64,112},{80,64},{96,80},{128,176},{144,128}... | collective-permute-start | bytes 73736 | tf_op jit(solution)/shard_map/ppermute | solution.py:214
  44.4 8.2 %collective-permute-start.1 = (f32[48,128]{1,0:T(8,128)S(1)}, f32[48,128]{1,0:T(8,128)S(1)}, u32[]{:S(2)}, u32[]{:S(2)}) collective-permute-start(f32[48,128]{1,0:T(8,128)S(1)} %pad_maximum_fusion.1.own_ref), channel_id=1, source_target_pairs={{0,32},{16,48},{32,0},{64,96},{80,112},{96,64},{128,160},{144,176}... | collective-permute-start | bytes 73736 | tf_op jit(solution)/shard_map/ppermute | solution.py:214
  47.2 5.5 %collective-permute-start = (f32[48,128]{1,0:T(8,128)S(1)}, f32[48,128]{1,0:T(8,128)S(1)}, u32[]{:S(2)}, u32[]{:S(2)}) collective-permute-start(f32[48,128]{1,0:T(8,128)S(1)} %pad_maximum_fusion.1.own_ref), channel_id=1, source_target_pairs={{0,16},{16,32},{32,48},{64,80},{80,96},{96,112},{128,144},{144,160... | collective-permute-start | bytes 73736 | tf_op jit(solution)/shard_map/ppermute | solution.py:214
  52.5 9.6 %copy-start.1 = (f32[2,128,4,128]{3,2,1,0:T(4,128)S(1)}, f32[2,128,4,128]{3,2,1,0:T(4,128)}, u32[]{:S(2)}) copy-start(f32[2,128,4,128]{3,2,1,0:T(4,128)} %param.1) | copy-start | bytes 1572868
  52.5 0.6 copy-start.4
  52.5 0.6 copy-start.5
  53.1 0.6 copy-start.6
  55.3 19.4 %all-to-all-start.2 = ((f32[8,96,128]{2,1,0:T(8,128)}), f32[8,96,128]{2,1,0:T(8,128)S(1)}, u32[]{:S(2)}, u32[]{:S(2)}) async-start(f32[8,96,128]{2,1,0:T(8,128)} %pack.1), calls=%async_computation.2 | async-start | bytes 786432 | tf_op jit(solution)/shard_map/all_to_all | solution.py:216
  62.2 17.6 %collective-permute-start.3 = (f32[256,128]{1,0:T(8,128)S(1)}, f32[256,128]{1,0:T(8,128)S(1)}, u32[]{:S(2)}, u32[]{:S(2)}) collective-permute-start(f32[256,128]{1,0:T(8,128)S(1)} %bitcast.25), channel_id=1, source_target_pairs={{0,8},{1,9},{2,10},{16,24},{17,25},{18,26},{32,40},{33,41},{34,42}... | collective-permute-start | bytes 393224 | tf_op jit(solution)/shard_map/ppermute | solution.py:195
  74.7 1.1 copy-start.2
  75.8 40.3 %all-to-all-start.4 = ((f32[4,512,128]{2,1,0:T(8,128)}), f32[4,512,128]{2,1,0:T(8,128)S(1)}, u32[]{:S(2)}, u32[]{:S(2)}) async-start(f32[4,512,128]{2,1,0:T(8,128)} %broadcast_in_dim.26), calls=%async_computation.4 | async-start | bytes 2097152 | tf_op jit(solution)/shard_map/all_to_all | solution.py:180
  79.9 0.7 collective-permute-start.4
  80.6 11.9 %collective-permute-start.5 = (f32[256,128]{1,0:T(8,128)S(1)}, f32[256,128]{1,0:T(8,128)S(1)}, u32[]{:S(2)}, u32[]{:S(2)}) collective-permute-start(f32[256,128]{1,0:T(8,128)S(1)} %broadcast_select_fusion.1), channel_id=1, source_target_pairs={{0,2},{1,3},{2,0},{4,6},{5,7},{6,4},{8,10},{9,11},{10,8},{12,14},{... | collective-permute-start | bytes 393224 | tf_op jit(solution)/shard_map/ppermute | solution.py:202
  116.1 1.0 copy-start

commit v3 on v2

--- a/solution.py
+++ b/solution.py
@@ -12,7 +12,6 @@
 NX = 4
 NZ = 8
 PART = NB // NZ
-UPPER = [(i, j) for i in range(PANELS) for j in range(i, PANELS)]
 VMEM = pl.BlockSpec(memory_space=pltpu.VMEM)
 SMEM = pl.BlockSpec(memory_space=pltpu.SMEM)
 
@@ -49,10 +48,14 @@
     eye = lax.broadcasted_iota(jnp.int32, (NB, NB), 0) == lax.broadcasted_iota(jnp.int32, (NB, NB), 1)
     eye = eye.astype(jnp.float32)
     zero = jnp.zeros((NB, NB), jnp.float32)
-    for k in range(PANELS):
-        for q, j in zip((0, 2, 3), (k, k + 1, k + 2)):
-            tile = lead_ref[:, UPPER.index((k, j)) * PART :, :][:, :PART, :].reshape(NB, NB) if j < PANELS else zero
-            work[k, :, q * NB : (q + 1) * NB] = tile
+
+    def tile(core, n):
+        return lead_ref[core, :, n * PART : (n + 1) * PART, :].reshape(NB, NB)
+
+    rows = ((tile(0, 0), tile(1, 0), tile(0, 1)), (tile(1, 1), tile(1, 2).T, zero), (tile(0, 2), zero, zero))
+    for k, tiles in enumerate(rows):
+        for q, value in zip((0, 2, 3), tiles):
+            work[k, :, q * NB : (q + 1) * NB] = value
         work[k, :, NB : 2 * NB] = eye
 
     def panel(k, carry):
@@ -113,41 +116,49 @@
     )
 
 
-def pack_kernel(place_ref, own_ref, one_ref, two_ref, three_ref, out_ref, got):
-    for d, ref in enumerate((own_ref, one_ref, two_ref, three_ref)):
-        got[d] = ref[...]
-    my_x = lax.rem(place_ref[0], NX)
-    for p, (i, j) in enumerate(UPPER):
-        tile = got[lax.rem(my_x + NX - i, NX), j * PART : (j + 1) * PART, :]
+def pack_lead_kernel(got_ref, lead_ref):
+    core = lax.rem(lax.axis_index("col"), 2)
+    for n, block in enumerate((0, core, 2)):
+        at = pl.multiple_of((0 if n == 0 else 1 - core) * PART, PART)
+        tile = got_ref[block, pl.ds(at, PART), :]
         for z in range(NZ):
-            out_ref[z, p * PART : (p + 1) * PART, :] = tile
-
-
-def pack(place, pieces):
-    shape = pieces[0].shape
+            lead_ref[z, n * PART : (n + 1) * PART, :] = tile
+
+
+def pack_cols_kernel(got_ref, cols_ref):
+    size = got_ref.shape[1] - 2 * PART
+    for i in range(PANELS):
+        tile = got_ref[i, 2 * PART :, :]
+        for z in range(NZ):
+            cols_ref[z, i * size : (i + 1) * size, :] = tile
+
+
+def pack(kernel, got, rows):
     return pl.pallas_call(
-        pack_kernel,
-        out_shape=jax.ShapeDtypeStruct((NZ, len(UPPER) * PART, NB), jnp.float32),
-        in_specs=[SMEM] + [VMEM] * len(pieces),
-        out_specs=VMEM,
-        scratch_shapes=[pltpu.VMEM((len(pieces),) + shape, jnp.float32)],
-        name="pack",
-    )(place, *pieces)
-
-
-def finish_kernel(place_ref, inv_ref, low_ref, x_ref, y_ref, m_ref, out_ref):
-    my_row = place_ref[0]
-    my_col = place_ref[1]
-    col_count = place_ref[2]
+        kernel, out_shape=jax.ShapeDtypeStruct((NZ, rows, NB), jnp.float32), in_specs=[VMEM], out_specs=VMEM
+    )(got)
+
+
+def finish_kernel(inv_ref, low_ref, mine_ref, other_ref, y_ref, m_ref, out_ref, x_got):
+    my_row = lax.axis_index("row")
+    my_col = lax.axis_index("col")
+    col_count = lax.axis_size("col")
     row_count = NX * NZ
+    core = lax.rem(my_col, 2)
     odd = lax.rem(my_col // 2, 2)
-    left = [x_ref[0, odd], x_ref[1, odd], x_ref[0, 1 - odd]]
+    x_got[core] = mine_ref[...]
+    x_got[1 - core] = other_ref[...]
+    left = [x_got[0, odd], x_got[1, odd], x_got[0, 1 - odd]]
     rows0 = mm_nt(left[0], inv_ref[0])
     rows1 = mm_nt(left[1] - mm_nt(rows0, low_ref[0, 0]), inv_ref[1])
     rows2 = mm_nt(left[2] - mm_nt(rows0, low_ref[0, 1]) - mm_nt(rows1, low_ref[1, 0]), inv_ref[2])
     right = []
     for i in range(PANELS):
-        right.append(jnp.concatenate([y_ref[i, pl.ds(s, NB, stride=4), :] for s in range(4)], axis=1))
+        tiles = []
+        for s in range(4):
+            at = i * PART * 4 + s
+            tiles.append(jnp.concatenate([y_ref[z, pl.ds(at, PART, stride=4), :] for z in range(NZ)], axis=0))
+        right.append(jnp.concatenate(tiles, axis=1))
     cols0 = mm(inv_ref[0], right[0])
     cols1 = mm(inv_ref[1], right[1] - mm(low_ref[0, 0], cols0))
     cols2 = mm(inv_ref[2], right[2] - mm(low_ref[0, 1], cols0) - mm(low_ref[1, 0], cols1))
@@ -165,14 +176,15 @@
             out_ref[t, pl.ds(s, NB, stride=4), :] = jnp.where(below + u >= v, value, 0.0)
 
 
-def finish(place, inverse, low, x_part, y_part, matrix):
+def finish(inverse, low, mine, other, y_part, matrix):
     return pl.pallas_call(
         finish_kernel,
         out_shape=jax.ShapeDtypeStruct(matrix.shape, jnp.float32),
-        in_specs=[SMEM] + [VMEM] * 5,
+        in_specs=[VMEM] * 6,
         out_specs=VMEM,
+        scratch_shapes=[pltpu.VMEM((2,) + mine.shape, jnp.float32)],
         name="finish",
-    )(place, inverse, low, x_part, y_part, matrix)
+    )(inverse, low, mine, other, y_part, matrix)
 
 
 def to_all(value, axis, groups):
@@ -184,9 +196,9 @@
     tile_rows, nb, tile_cols, _ = covariance.shape
     col_count = lax.axis_size("col")
     my_col = lax.axis_index("col")
-    place = jnp.stack([lax.axis_index("row"), my_col, jnp.int32(col_count)])
     matrix = covariance.reshape(tile_rows, nb * tile_cols, nb)
     along_z = [[z * NX + x for z in range(NZ)] for x in range(NX)]
+    along_x = [[z * NX + x for x in range(NX)] for z in range(NZ)]
     along_y = [[c for c in range(q, col_count, 2)] for q in range(2)]
     pairs = [[c, c + 1] for c in range(0, col_count, 2)]
     half, quarter = col_count // 2, col_count // 4
@@ -200,24 +212,20 @@
     for start in range(0, col_count, quarter):
         steps += [(start, start + 2), (start + 1, start + 3), (start + 2, start)]
     near = lax.ppermute(mine, "col", steps)
-    x_part = lax.all_gather(jnp.stack([mine, near]), "col", axis_index_groups=pairs)
+    panels = jnp.stack([mine, near])
+    other = lax.ppermute(panels, "col", [(c, c ^ 1) for c in range(col_count)])
 
     piece = lax.all_to_all(matrix[0].reshape(NZ, PART * tile_cols, nb), "row", 0, 0, axis_index_groups=along_z)[0]
-    y_block = to_all(piece, "row", along_z).reshape(nb * tile_cols, nb)
     head = piece.reshape(PART, tile_cols, nb)[:, 0, :]
     own = to_all(head, "col", along_y)[:2]
-    both = lax.all_gather(own, "col", axis_index_groups=pairs)
-    lead = jnp.concatenate([both[j % 2, j // 2] for j in range(PANELS)], axis=0)
-    pieces = [lead]
-    for d in range(1, NX):
-        hops = [(z * NX + x, z * NX + (x + d) % NX) for z in range(NZ) for x in range(PANELS)]
-        pieces.append(lax.ppermute(lead, "row", hops))
-    lead = pack(place, pieces)
+    got = to_all(jnp.concatenate([own.reshape(2 * PART, nb), piece], axis=0), "row", along_x)
+    lead = pack(pack_lead_kernel, got, PANELS * PART)
     lead = lax.all_to_all(lead, "row", 0, 0, axis_index_groups=along_z)
-    along_x = [[z * NX + x for x in range(NX)] for z in range(NZ)]
-    y_part = to_all(y_block, "row", along_x)
+    lead = lax.all_gather(lead, "col", axis_index_groups=pairs)
+    cols = pack(pack_cols_kernel, got, PANELS * PART * tile_cols)
+    y_part = lax.all_to_all(cols, "row", 0, 0, axis_index_groups=along_z)
     inverse, low = factor(lead)
-    out = finish(place, inverse, low, x_part, y_part, matrix)
+    out = finish(inverse, low, panels, other, y_part, matrix)
     return out.reshape(covariance.shape)
 
 

time: 124 us -> 115 us (0.927)
  the two profiles are of different devices: /device:TPU:27 before, /device:TPU:57 now
where the time goes in v3:
time: 115 us; the launch traced here: 114 us
  blocking collectives  42.2 us (37%)
  Pallas kernels  24.1 us (21%)
  starting transfers between devices  23.5 us (20%)
  waiting for transfers between devices  22.3 us (19%)
  local copies, waits for them, and re-layouts  2.06 us (2%)
    all_to_all x1, blocking collectives, per_device(): lax.all_to_all(matrix[0].reshape(NZ, PART * tile_cols, nb), 'row', 0, 0,...  20.3 us
    all_to_all x2, blocking collectives, to_all(): lax.all_to_all(jnp.broadcast_to(value[None], (count,) + value.shape), axi...  19.7 us
    ppermute x1, waiting for transfers between devices, per_device(): near = lax.ppermute(mine, 'col', steps)  15.7 us
    pallas_call x1, Pallas kernels, factor(): pl.pallas_call(factor_kernel, out_shape=(jax.ShapeDtypeStruct((PANELS, NB...  14.2 us
    ppermute x1, starting transfers between devices, per_device(): other = lax.ppermute(panels, 'col', [(c, c ^ 1) for c in range(col_count)])  14 us
    all_to_all x1, waiting for transfers between devices, per_device(): lead = lax.all_to_all(lead, 'row', 0, 0, axis_index_groups=along_z)  6.66 us
    pallas_call x1, Pallas kernels, finish(): pl.pallas_call(finish_kernel, out_shape=jax.ShapeDtypeStruct(matrix.shape...  6.34 us
    all_to_all x1, starting transfers between devices, per_device(): y_part = lax.all_to_all(cols, 'row', 0, 0, axis_index_groups=along_z)  3.55 us
  transfers between devices with their start and end apart: 6, of which 2 were waited for; matrix products, arithmetic and copies ran while one was open for 0% of the time, Pallas kernels for 14%

profile of v3, /device:TPU:57, one launch (start us, length us, event | category | flops | bytes accessed | tf_op | source)
XLA Modules:
  0.0 114.4 jit_solution(2635549614828310154)
XLA Ops:
  0.0 0.0 slice-start
  0.0 0.9 slice-done
  1.0 20.3 %all_to_all.25 = f32[8,64,128]{2,1,0:T(8,128)S(1)} all-to-all(f32[8,64,128]{2,1,0:T(8,128)S(1)} %bitcast.13), channel_id=1, replica_groups={{0,64,128,192,256,320,384,448},{16,80,144,208,272,336,400,464},{32,96,1..., dimensions={0} | all-to-all | bytes 524288 | tf_op jit(solution)/shard_map/all_to_all | solution.py:218
  21.3 10.6 %all_to_all.26 = f32[8,16,128]{2,1,0:T(8,128)S(1)} all-to-all(f32[8,16,128]{2,1,0:T(8,128)S(1)} %broadcast_in_dim.14), channel_id=1, replica_groups={{0,2,4,6,8,10,12,14},{1,3,5,7,9,11,13,15},{16,18,20,22,24,26,28,30},{17..., dimensions={0} | all-to-all | bytes 131072 | tf_op jit(solution)/shard_map/all_to_all | solution.py:192
  31.9 9.1 %all_to_all.27.got_ref = f32[4,96,128]{2,1,0:T(8,128)} all-to-all(f32[4,96,128]{2,1,0:T(8,128)S(1)} %broadcast_in_dim.15), channel_id=1, replica_groups={{0,16,32,48},{64,80,96,112},{128,144,160,176},{192,208,224,240},{256,27..., dimensions={0} | all-to-all | bytes 393216 | tf_op jit(solution)/shard_map/all_to_all | solution.py:192
  41.0 1.6 %shard_map.17 = f32[8,48,128]{2,1,0:T(8,128)} custom-call(f32[4,96,128]{2,1,0:T(8,128)} %all_to_all.27.got_ref), custom_call_target="tpu_custom_call" | custom-call | tf_op jit(solution)/shard_map/pallas_call | solution.py:137
  42.6 3.4 %all-to-all-start.3 = ((f32[8,48,128]{2,1,0:T(8,128)}), f32[8,48,128]{2,1,0:T(8,128)S(1)}, u32[]{:S(2)}, u32[]{:S(2)}) async-start(f32[8,48,128]{2,1,0:T(8,128)} %shard_map.17), calls=%async_computation.3 | async-start | bytes 393216 | tf_op jit(solution)/shard_map/all_to_all | solution.py:223
  46.0 1.9 %shard_map.18 = f32[8,192,128]{2,1,0:T(8,128)} custom-call(f32[4,96,128]{2,1,0:T(8,128)} %all_to_all.27.got_ref), custom_call_target="tpu_custom_call" | custom-call | tf_op jit(solution)/shard_map/pallas_call | solution.py:137
  47.9 0.0 copy-start.1
  47.9 6.7 %all-to-all-done.3 = f32[8,48,128]{2,1,0:T(8,128)S(1)} async-done(((f32[8,48,128]{2,1,0:T(8,128)}), f32[8,48,128]{2,1,0:T(8,128)S(1)}, u32[]{:S(2)}, u32[]{:S(2)}) %all-to-all-start.3) | async-done | bytes 196640 | tf_op jit(solution)/shard_map/all_to_all | solution.py:223
  54.6 3.5 %all-to-all-start.4 = ((f32[8,192,128]{2,1,0:T(8,128)}), f32[8,192,128]{2,1,0:T(8,128)S(1)}, u32[]{:S(2)}, u32[]{:S(2)}) async-start(f32[8,192,128]{2,1,0:T(8,128)} %shard_map.18), calls=%async_computation.4 | async-start | bytes 1572864 | tf_op jit(solution)/shard_map/all_to_all | solution.py:226
  58.1 0.0 copy-done.1
  58.1 0.1 slice.20
  58.2 0.7 collective-permute-start
  58.9 0.0 collective-permute-done
  59.0 0.7 collective-permute-start.1
  59.6 0.0 collective-permute-done.1
  59.7 1.3 %collective-permute-start.2 = (f32[256,128]{1,0:T(8,128)S(1)}, f32[256,128]{1,0:T(8,128)S(1)}, u32[]{:S(2)}, u32[]{:S(2)}) collective-permute-start(f32[256,128]{1,0:T(8,128)S(1)} %broadcast_select_fusion.1), channel_id=1, source_target_pairs={{0,2},{1,3},{2,0},{4,6},{5,7},{6,4},{8,10},{9,11},{10,8},{12,14},{... | collective-permute-start | bytes 393224 | tf_op jit(solution)/shard_map/ppermute | solution.py:214
  61.0 15.7 %collective-permute-done.2 = f32[256,128]{1,0:T(8,128)S(1)} collective-permute-done((f32[256,128]{1,0:T(8,128)S(1)}, f32[256,128]{1,0:T(8,128)S(1)}, u32[]{:S(2)}, u32[]{:S(2)}) %collective-permute-start.2) | collective-permute-done | bytes 131104 | tf_op jit(solution)/shard_map/ppermute | solution.py:214
  76.7 0.0 copy-start.2
  76.7 14.0 %collective-permute-start.3 = (f32[2,256,128]{2,1,0:T(8,128)S(1)}, f32[2,256,128]{2,1,0:T(8,128)S(1)}, u32[]{:S(2)}, u32[]{:S(2)}) collective-permute-start(f32[2,256,128]{2,1,0:T(8,128)S(1)} %pad_maximum_fusion.mine_ref), channel_id=1, source_target_pairs={{0,1},{1,0},{2,3},{3,2},{4,5},{5,4},{6,7},{7,6},{8,9},{9,8},{10,11... | collective-permute-start | bytes 786440 | tf_op jit(solution)/shard_map/ppermute | solution.py:216
  90.6 2.2 %all-gather = f32[16,48,128]{2,1,0:T(8,128)} all-gather(f32[8,48,128]{2,1,0:T(8,128)S(1)} %all-to-all-done.3), channel_id=2, replica_groups={{0,1},{2,3},{4,5},{6,7},{8,9},{10,11},{12,13},{14,15},{16,17},{18,19},{..., dimensions={0}, use_global_device_ids=true | all-gather | bytes 589824 | tf_op jit(solution)/shard_map/all_gather | solution.py:224
  92.9 0.0 copy-done.2
  92.9 14.2 %factor.1 = (f32[3,128,128]{2,1,0:T(8,128)}, f32[2,2,128,128]{3,2,1,0:T(8,128)}) custom-call(f32[2,8,48,128]{3,2,1,0:T(8,128)} %bitcast.14), custom_call_target="tpu_custom_call" | custom-call | tf_op jit(solution)/shard_map/factor/pallas_call | solution.py:97
  107.1 0.0 collective-permute-done.3.other_ref
  107.1 0.0 copy-start.3
  107.1 0.0 all-to-all-done.4.y_ref
  107.1 0.0 copy-start
  107.1 0.7 copy-done.3
  107.8 0.3 copy-done
  108.1 6.3 %finish.1 = f32[2,512,128]{2,1,0:T(8,128)} custom-call(f32[3,128,128]{2,1,0:T(8,128)} %get-tuple-element.7.inv_ref, f32[2,2,128,128]{3,2,1,0:T(8,128)} %get-tuple-element.8.low_ref, f32[2,256,128]{2,1,0:T(8,128)} %copy-done.2, f32[2,256,128]{2,1,0:T(8,128)} %copy-done.3, f32[8,192,128]{2,1,0:T(8,128)} %copy-done, f32[2,512,128]{2,1,0:T(8,128)} %bitcast.12), custom_call_target="tpu_custom_call" | custom-call | tf_op jit(solution)/shard_map/finish/pallas_call | solution.py:180
  (9 shorter events, 0.1 us)
Async XLA Ops:
  0.0 0.9 slice-start
  42.6 11.9 %all-to-all-start.3 = ((f32[8,48,128]{2,1,0:T(8,128)}), f32[8,48,128]{2,1,0:T(8,128)S(1)}, u32[]{:S(2)}, u32[]{:S(2)}) async-start(f32[8,48,128]{2,1,0:T(8,128)} %shard_map.17), calls=%async_computation.3 | async-start | bytes 393216 | tf_op jit(solution)/shard_map/all_to_all | solution.py:223
  47.9 10.2 %copy-start.1 = (f32[2,128,4,128]{3,2,1,0:T(4,128)S(1)}, f32[2,128,4,128]{3,2,1,0:T(4,128)}, u32[]{:S(2)}) copy-start(f32[2,128,4,128]{3,2,1,0:T(4,128)} %param.1) | copy-start | bytes 1572868
  54.6 52.5 %all-to-all-start.4 = ((f32[8,192,128]{2,1,0:T(8,128)}), f32[8,192,128]{2,1,0:T(8,128)S(1)}, u32[]{:S(2)}, u32[]{:S(2)}) async-start(f32[8,192,128]{2,1,0:T(8,128)} %shard_map.18), calls=%async_computation.4 | async-start | bytes 1572864 | tf_op jit(solution)/shard_map/all_to_all | solution.py:226
  58.2 0.7 collective-permute-start
  59.0 0.7 collective-permute-start.1
  59.7 17.0 %collective-permute-start.2 = (f32[256,128]{1,0:T(8,128)S(1)}, f32[256,128]{1,0:T(8,128)S(1)}, u32[]{:S(2)}, u32[]{:S(2)}) collective-permute-start(f32[256,128]{1,0:T(8,128)S(1)} %broadcast_select_fusion.1), channel_id=1, source_target_pairs={{0,2},{1,3},{2,0},{4,6},{5,7},{6,4},{8,10},{9,11},{10,8},{12,14},{... | collective-permute-start | bytes 393224 | tf_op jit(solution)/shard_map/ppermute | solution.py:214
  76.7 16.2 %copy-start.2 = (f32[2,256,128]{2,1,0:T(8,128)}, f32[2,256,128]{2,1,0:T(8,128)S(1)}, u32[]{:S(2)}) copy-start(f32[2,256,128]{2,1,0:T(8,128)S(1)} %pad_maximum_fusion.mine_ref) | copy-start | bytes 786436
  76.7 30.4 %collective-permute-start.3 = (f32[2,256,128]{2,1,0:T(8,128)S(1)}, f32[2,256,128]{2,1,0:T(8,128)S(1)}, u32[]{:S(2)}, u32[]{:S(2)}) collective-permute-start(f32[2,256,128]{2,1,0:T(8,128)S(1)} %pad_maximum_fusion.mine_ref), channel_id=1, source_target_pairs={{0,1},{1,0},{2,3},{3,2},{4,5},{5,4},{6,7},{7,6},{8,9},{9,8},{10,11... | collective-permute-start | bytes 786440 | tf_op jit(solution)/shard_map/ppermute | solution.py:216
  107.1 0.7 copy-start.3
  107.1 1.0 copy-start

commit v4 on v3

--- a/solution.py
+++ b/solution.py
@@ -18,6 +18,18 @@
 
 def mm(a, b):
     return jnp.dot(a, b, precision=lax.Precision.HIGHEST, preferred_element_type=jnp.float32)
+
+
+def mm3(a, b, contract=(1, 0)):
+    a_high, b_high = a.astype(jnp.bfloat16), b.astype(jnp.bfloat16)
+    a_low = (a - a_high.astype(jnp.float32)).astype(jnp.bfloat16)
+    b_low = (b - b_high.astype(jnp.float32)).astype(jnp.bfloat16)
+    dims = (((contract[0],), (contract[1],)), ((), ()))
+
+    def dot(p, q):
+        return lax.dot_general(p, q, dims, preferred_element_type=jnp.float32)
+
+    return dot(a_high, b_high) + (dot(a_high, b_low) + dot(a_low, b_high))
 
 
 def factor_strip(strip, first):
@@ -69,11 +81,11 @@
                 pieces = [jnp.zeros((first, 4 * NB), jnp.float32)] if first else []
                 pieces += [solved, jnp.zeros((rest, 4 * NB), jnp.float32)]
                 padded = jnp.concatenate(pieces, axis=0)
-                below = work[k, first + STRIP :, :]
-                below = below - mm(below[:, :NB], padded)
-                strip = below[:STRIP]
+                strip = work[k, first + STRIP : first + 2 * STRIP, :]
+                strip = strip - mm3(strip[:, :NB], padded)
                 if rest > STRIP:
-                    work[k, first + 2 * STRIP :, :] = below[STRIP:]
+                    below = work[k, first + 2 * STRIP :, :]
+                    work[k, first + 2 * STRIP :, :] = below - mm3(below[:, :NB], padded)
         inv_ref[k] = upper[:, NB : 2 * NB]
 
         @pl.when(k < PANELS - 1)
@@ -110,19 +122,8 @@
     )(lead)
 
 
-def mm_nt(a, b):
-    return lax.dot_general(
-        a, b, (((1,), (1,)), ((), ())), precision=lax.Precision.HIGHEST, preferred_element_type=jnp.float32
-    )
-
-
-def pack_lead_kernel(got_ref, lead_ref):
-    core = lax.rem(lax.axis_index("col"), 2)
-    for n, block in enumerate((0, core, 2)):
-        at = pl.multiple_of((0 if n == 0 else 1 - core) * PART, PART)
-        tile = got_ref[block, pl.ds(at, PART), :]
-        for z in range(NZ):
-            lead_ref[z, n * PART : (n + 1) * PART, :] = tile
+def mm3_nt(a, b):
+    return mm3(a, b, (1, 1))
 
 
 def pack_cols_kernel(got_ref, cols_ref):
@@ -149,9 +150,9 @@
     x_got[core] = mine_ref[...]
     x_got[1 - core] = other_ref[...]
     left = [x_got[0, odd], x_got[1, odd], x_got[0, 1 - odd]]
-    rows0 = mm_nt(left[0], inv_ref[0])
-    rows1 = mm_nt(left[1] - mm_nt(rows0, low_ref[0, 0]), inv_ref[1])
-    rows2 = mm_nt(left[2] - mm_nt(rows0, low_ref[0, 1]) - mm_nt(rows1, low_ref[1, 0]), inv_ref[2])
+    rows0 = mm3_nt(left[0], inv_ref[0])
+    rows1 = mm3_nt(left[1] - mm3_nt(rows0, low_ref[0, 0]), inv_ref[1])
+    rows2 = mm3_nt(left[2] - mm3_nt(rows0, low_ref[0, 1]) - mm3_nt(rows1, low_ref[1, 0]), inv_ref[2])
     right = []
     for i in range(PANELS):
         tiles = []
@@ -159,17 +160,22 @@
             at = i * PART * 4 + s
             tiles.append(jnp.concatenate([y_ref[z, pl.ds(at, PART, stride=4), :] for z in range(NZ)], axis=0))
         right.append(jnp.concatenate(tiles, axis=1))
-    cols0 = mm(inv_ref[0], right[0])
-    cols1 = mm(inv_ref[1], right[1] - mm(low_ref[0, 0], cols0))
-    cols2 = mm(inv_ref[2], right[2] - mm(low_ref[0, 1], cols0) - mm(low_ref[1, 0], cols1))
+    cols0 = mm3(inv_ref[0], right[0])
+    cols1 = mm3(inv_ref[1], right[1] - mm3(low_ref[0, 0], cols0))
+    cols2 = mm3(inv_ref[2], right[2] - mm3(low_ref[0, 1], cols0) - mm3(low_ref[1, 0], cols1))
     rows = jnp.concatenate([rows0, rows1, rows2], axis=1)
-    product = mm(rows, jnp.concatenate([cols0, cols1, cols2], axis=0))
+    cols = jnp.concatenate([cols0, cols1, cols2], axis=0)
     panel = jnp.where(my_col == 0, rows0, jnp.where(my_col == 1, rows1, rows2))
     u = lax.broadcasted_iota(jnp.int32, (NB, NB), 0)
     v = lax.broadcasted_iota(jnp.int32, (NB, NB), 1)
     for t in range(2):
+        live = min(4, -(-(t + 1) * row_count // col_count))
+        product = mm3(rows[t * NB : (t + 1) * NB], cols[:, : live * NB])
         for s in range(4):
-            value = m_ref[t, pl.ds(s, NB, stride=4), :] - product[t * NB : (t + 1) * NB, s * NB : (s + 1) * NB]
+            if s >= live:
+                out_ref[t, pl.ds(s, NB, stride=4), :] = jnp.zeros((NB, NB), jnp.float32)
+                continue
+            value = m_ref[t, pl.ds(s, NB, stride=4), :] - product[:, s * NB : (s + 1) * NB]
             if s == 0:
                 value = jnp.where(my_col < PANELS, panel[t * NB : (t + 1) * NB], value)
             below = (t * row_count + my_row - s * col_count - my_col) * NB
@@ -219,8 +225,14 @@
     head = piece.reshape(PART, tile_cols, nb)[:, 0, :]
     own = to_all(head, "col", along_y)[:2]
     got = to_all(jnp.concatenate([own.reshape(2 * PART, nb), piece], axis=0), "row", along_x)
-    lead = pack(pack_lead_kernel, got, PANELS * PART)
-    lead = lax.all_to_all(lead, "row", 0, 0, axis_index_groups=along_z)
+    first_core = my_col % 2 == 0
+    lead = [
+        got[0, :PART],
+        jnp.where(first_core, got[0, PART : 2 * PART], got[1, :PART]),
+        jnp.where(first_core, got[2, PART : 2 * PART], got[2, :PART]),
+    ]
+    lead = jnp.concatenate(lead, axis=0)
+    lead = to_all(lead, "row", along_z)
     lead = lax.all_gather(lead, "col", axis_index_groups=pairs)
     cols = pack(pack_cols_kernel, got, PANELS * PART * tile_cols)
     y_part = lax.all_to_all(cols, "row", 0, 0, axis_index_groups=along_z)

time: 115 us -> 112 us (0.974)
  blocking collectives: 42.2 us -> 33.1 us
  waiting for transfers between devices: 22.3 us -> 27.5 us
  Pallas kernels: 24.1 us -> 19.2 us
  starting transfers between devices: 23.5 us -> 27.5 us
  local copies, waits for them, and re-layouts: 2.06 us -> 3.45 us
    all_to_all x2 -> x1, blocking collectives: 19.7 us -> 10.6 us  [to_all(): lax.all_to_all(jnp.broadcast_to(value[None], (count,) + value.shape), axi...]
    all_to_all x1 -> x2, waiting for transfers between devices: 6.66 us -> 11.9 us  [to_all(): lax.all_to_all(jnp.broadcast_to(value[None], (count,) + value.shape), axi...]
    all_to_all x1 -> x2, starting transfers between devices: 3.39 us -> 7.41 us  [to_all(): lax.all_to_all(jnp.broadcast_to(value[None], (count,) + value.shape), axi...]
    pallas_call x1, Pallas kernels: 14.2 us -> 12.5 us  [factor(): pl.pallas_call(factor_kernel, out_shape=(jax.ShapeDtypeStruct((PANELS, NB...]
    pallas_call x2 -> x1, Pallas kernels: 3.5 us -> 1.87 us  [pack(): pl.pallas_call(kernel, out_shape=jax.ShapeDtypeStruct((NZ, rows, NB), jnp...]
    pallas_call x1, Pallas kernels: 6.34 us -> 4.86 us  [finish(): pl.pallas_call(finish_kernel, out_shape=jax.ShapeDtypeStruct(matrix.shape...]
    broadcast_in_dim x2 -> x3, local copies, waits for them, and re-layouts: 0.02 us -> 1.43 us  [to_all(): jnp.broadcast_to(value[None], (count,) + value.shape)]
  transfers between devices with their start and end apart: 6 -> 7, of which waited for: 2 -> 3; matrix products, arithmetic and copies ran while one was open for 0% -> 0% of each run, Pallas kernels for 14% -> 13%
where the time goes in v4:
time: 112 us; the launch traced here: 111 us
  blocking collectives  33.1 us (30%)
  starting transfers between devices  27.5 us (25%)
  waiting for transfers between devices  27.5 us (25%)
  Pallas kernels  19.2 us (17%)
  local copies, waits for them, and re-layouts  3.45 us (3%)
    all_to_all x1, blocking collectives, per_device(): lax.all_to_all(matrix[0].reshape(NZ, PART * tile_cols, nb), 'row', 0, 0,...  20.3 us
    ppermute x1, waiting for transfers between devices, per_device(): near = lax.ppermute(mine, 'col', steps)  15.7 us
    ppermute x1, starting transfers between devices, per_device(): other = lax.ppermute(panels, 'col', [(c, c ^ 1) for c in range(col_count)])  14 us
    pallas_call x1, Pallas kernels, factor(): pl.pallas_call(factor_kernel, out_shape=(jax.ShapeDtypeStruct((PANELS, NB...  12.5 us
    all_to_all x2, waiting for transfers between devices, to_all(): lax.all_to_all(jnp.broadcast_to(value[None], (count,) + value.shape), axi...  11.9 us
    all_to_all x1, blocking collectives, to_all(): lax.all_to_all(jnp.broadcast_to(value[None], (count,) + value.shape), axi...  10.6 us
    all_to_all x2, starting transfers between devices, to_all(): lax.all_to_all(jnp.broadcast_to(value[None], (count,) + value.shape), axi...  7.41 us
    pallas_call x1, Pallas kernels, finish(): pl.pallas_call(finish_kernel, out_shape=jax.ShapeDtypeStruct(matrix.shape...  4.86 us
  transfers between devices with their start and end apart: 7, of which 3 were waited for; matrix products, arithmetic and copies ran while one was open for 0% of the time, Pallas kernels for 13%

profile of v4, /device:TPU:57, one launch (start us, length us, event | category | flops | bytes accessed | tf_op | source)
XLA Modules:
  0.0 111.1 jit_solution(10876338844356442568)
XLA Ops:
  0.0 0.0 slice-start
  0.0 0.9 slice-done
  1.0 20.3 %all_to_all.25 = f32[8,64,128]{2,1,0:T(8,128)S(1)} all-to-all(f32[8,64,128]{2,1,0:T(8,128)S(1)} %bitcast.19), channel_id=1, replica_groups={{0,64,128,192,256,320,384,448},{16,80,144,208,272,336,400,464},{32,96,1..., dimensions={0} | all-to-all | bytes 524288 | tf_op jit(solution)/shard_map/all_to_all | solution.py:224
  21.3 10.6 %all_to_all.26 = f32[8,16,128]{2,1,0:T(8,128)S(1)} all-to-all(f32[8,16,128]{2,1,0:T(8,128)S(1)} %broadcast_in_dim.9), channel_id=1, replica_groups={{0,2,4,6,8,10,12,14},{1,3,5,7,9,11,13,15},{16,18,20,22,24,26,28,30},{17..., dimensions={0} | all-to-all | bytes 131072 | tf_op jit(solution)/shard_map/all_to_all | solution.py:198
  31.9 0.7 broadcast_in_dim.10
  32.6 4.0 %all-to-all-start.2 = ((f32[4,96,128]{2,1,0:T(8,128)}), f32[4,96,128]{2,1,0:T(8,128)S(1)}, u32[]{:S(2)}, u32[]{:S(2)}) async-start(f32[4,96,128]{2,1,0:T(8,128)} %broadcast_in_dim.10), calls=%async_computation.2 | async-start | bytes 393216 | tf_op jit(solution)/shard_map/all_to_all | solution.py:198
  36.6 5.2 %all-to-all-done.2.got_ref = f32[4,96,128]{2,1,0:T(8,128)S(1)} async-done(((f32[4,96,128]{2,1,0:T(8,128)}), f32[4,96,128]{2,1,0:T(8,128)S(1)}, u32[]{:S(2)}, u32[]{:S(2)}) %all-to-all-start.2) | async-done | bytes 196640 | tf_op jit(solution)/shard_map/all_to_all | solution.py:198
  41.8 0.7 broadcast_in_dim.22
  42.5 0.0 copy-done.3
  42.5 3.4 %all-to-all-start.3 = ((f32[8,48,128]{2,1,0:T(8,128)}), f32[8,48,128]{2,1,0:T(8,128)S(1)}, u32[]{:S(2)}, u32[]{:S(2)}) async-start(f32[8,48,128]{2,1,0:T(8,128)} %broadcast_in_dim.22), calls=%async_computation.3 | async-start | bytes 393216 | tf_op jit(solution)/shard_map/all_to_all | solution.py:198
  45.9 1.9 %shard_map.17 = f32[8,192,128]{2,1,0:T(8,128)} custom-call(f32[4,96,128]{2,1,0:T(8,128)} %copy-done.3), custom_call_target="tpu_custom_call" | custom-call | tf_op jit(solution)/shard_map/pallas_call | solution.py:138
  47.8 6.7 %all-to-all-done.3 = f32[8,48,128]{2,1,0:T(8,128)S(1)} async-done(((f32[8,48,128]{2,1,0:T(8,128)}), f32[8,48,128]{2,1,0:T(8,128)S(1)}, u32[]{:S(2)}, u32[]{:S(2)}) %all-to-all-start.3) | async-done | bytes 196640 | tf_op jit(solution)/shard_map/all_to_all | solution.py:198
  54.5 3.5 %all-to-all-start.4 = ((f32[8,192,128]{2,1,0:T(8,128)}), f32[8,192,128]{2,1,0:T(8,128)S(1)}, u32[]{:S(2)}, u32[]{:S(2)}) async-start(f32[8,192,128]{2,1,0:T(8,128)} %shard_map.17), calls=%async_computation.4 | async-start | bytes 1572864 | tf_op jit(solution)/shard_map/all_to_all | solution.py:238
  58.0 0.0 copy-done.1
  58.0 0.1 slice.40
  58.1 0.7 collective-permute-start
  58.8 0.0 collective-permute-done
  58.9 0.7 collective-permute-start.1
  59.5 0.0 collective-permute-done.1
  59.6 1.3 %collective-permute-start.2 = (f32[256,128]{1,0:T(8,128)S(1)}, f32[256,128]{1,0:T(8,128)S(1)}, u32[]{:S(2)}, u32[]{:S(2)}) collective-permute-start(f32[256,128]{1,0:T(8,128)S(1)} %broadcast_select_fusion.1), channel_id=1, source_target_pairs={{0,2},{1,3},{2,0},{4,6},{5,7},{6,4},{8,10},{9,11},{10,8},{12,14},{... | collective-permute-start | bytes 393224 | tf_op jit(solution)/shard_map/ppermute | solution.py:220
  60.9 15.7 %collective-permute-done.2 = f32[256,128]{1,0:T(8,128)S(1)} collective-permute-done((f32[256,128]{1,0:T(8,128)S(1)}, f32[256,128]{1,0:T(8,128)S(1)}, u32[]{:S(2)}, u32[]{:S(2)}) %collective-permute-start.2) | collective-permute-done | bytes 131104 | tf_op jit(solution)/shard_map/ppermute | solution.py:220
  76.6 0.0 copy-start.2
  76.6 14.0 %collective-permute-start.3 = (f32[2,256,128]{2,1,0:T(8,128)S(1)}, f32[2,256,128]{2,1,0:T(8,128)S(1)}, u32[]{:S(2)}, u32[]{:S(2)}) collective-permute-start(f32[2,256,128]{2,1,0:T(8,128)S(1)} %pad_maximum_fusion.mine_ref), channel_id=1, source_target_pairs={{0,1},{1,0},{2,3},{3,2},{4,5},{5,4},{6,7},{7,6},{8,9},{9,8},{10,11... | collective-permute-start | bytes 786440 | tf_op jit(solution)/shard_map/ppermute | solution.py:222
  90.5 2.2 %all-gather = f32[16,48,128]{2,1,0:T(8,128)} all-gather(f32[8,48,128]{2,1,0:T(8,128)S(1)} %all-to-all-done.3), channel_id=2, replica_groups={{0,1},{2,3},{4,5},{6,7},{8,9},{10,11},{12,13},{14,15},{16,17},{18,19},{..., dimensions={0}, use_global_device_ids=true | all-gather | bytes 589824 | tf_op jit(solution)/shard_map/all_gather | solution.py:236
  92.8 0.0 copy-done.2
  92.8 12.5 %factor.1 = (f32[3,128,128]{2,1,0:T(8,128)}, f32[2,2,128,128]{3,2,1,0:T(8,128)}) custom-call(f32[2,8,48,128]{3,2,1,0:T(8,128)} %bitcast.20), custom_call_target="tpu_custom_call" | custom-call | tf_op jit(solution)/shard_map/factor/pallas_call | solution.py:109
  105.3 0.0 collective-permute-done.3.other_ref
  105.3 0.0 all-to-all-done.4.y_ref
  105.3 0.0 copy-start
  105.3 0.7 copy-done.4
  106.0 0.3 copy-done
  106.2 4.9 %finish.1 = f32[2,512,128]{2,1,0:T(8,128)} custom-call(f32[3,128,128]{2,1,0:T(8,128)} %get-tuple-element.7.inv_ref, f32[2,2,128,128]{3,2,1,0:T(8,128)} %get-tuple-element.8.low_ref, f32[2,256,128]{2,1,0:T(8,128)} %copy-done.2, f32[2,256,128]{2,1,0:T(8,128)} %copy-done.4, f32[8,192,128]{2,1,0:T(8,128)} %copy-done, f32[2,512,128]{2,1,0:T(8,128)} %bitcast.18), custom_call_target="tpu_custom_call" | custom-call | tf_op jit(solution)/shard_map/finish/pallas_call | solution.py:186
  (13 shorter events, 0.1 us)
Async XLA Ops:
  0.0 0.9 slice-start
  32.6 9.2 %all-to-all-start.2 = ((f32[4,96,128]{2,1,0:T(8,128)}), f32[4,96,128]{2,1,0:T(8,128)S(1)}, u32[]{:S(2)}, u32[]{:S(2)}) async-start(f32[4,96,128]{2,1,0:T(8,128)} %broadcast_in_dim.10), calls=%async_computation.2 | async-start | bytes 393216 | tf_op jit(solution)/shard_map/all_to_all | solution.py:198
  41.8 0.7 copy-start.3
  42.5 11.9 %all-to-all-start.3 = ((f32[8,48,128]{2,1,0:T(8,128)}), f32[8,48,128]{2,1,0:T(8,128)S(1)}, u32[]{:S(2)}, u32[]{:S(2)}) async-start(f32[8,48,128]{2,1,0:T(8,128)} %broadcast_in_dim.22), calls=%async_computation.3 | async-start | bytes 393216 | tf_op jit(solution)/shard_map/all_to_all | solution.py:198
  47.8 10.2 %copy-start.1 = (f32[2,128,4,128]{3,2,1,0:T(4,128)S(1)}, f32[2,128,4,128]{3,2,1,0:T(4,128)}, u32[]{:S(2)}) copy-start(f32[2,128,4,128]{3,2,1,0:T(4,128)} %param.1) | copy-start | bytes 1572868
  54.5 50.8 %all-to-all-start.4 = ((f32[8,192,128]{2,1,0:T(8,128)}), f32[8,192,128]{2,1,0:T(8,128)S(1)}, u32[]{:S(2)}, u32[]{:S(2)}) async-start(f32[8,192,128]{2,1,0:T(8,128)} %shard_map.17), calls=%async_computation.4 | async-start | bytes 1572864 | tf_op jit(solution)/shard_map/all_to_all | solution.py:238
  58.1 0.7 collective-permute-start
  58.9 0.7 collective-permute-start.1
  59.6 17.0 %collective-permute-start.2 = (f32[256,128]{1,0:T(8,128)S(1)}, f32[256,128]{1,0:T(8,128)S(1)}, u32[]{:S(2)}, u32[]{:S(2)}) collective-permute-start(f32[256,128]{1,0:T(8,128)S(1)} %broadcast_select_fusion.1), channel_id=1, source_target_pairs={{0,2},{1,3},{2,0},{4,6},{5,7},{6,4},{8,10},{9,11},{10,8},{12,14},{... | collective-permute-start | bytes 393224 | tf_op jit(solution)/shard_map/ppermute | solution.py:220
  76.6 16.2 %copy-start.2 = (f32[2,256,128]{2,1,0:T(8,128)}, f32[2,256,128]{2,1,0:T(8,128)S(1)}, u32[]{:S(2)}) copy-start(f32[2,256,128]{2,1,0:T(8,128)S(1)} %pad_maximum_fusion.mine_ref) | copy-start | bytes 786436
  76.6 28.7 %collective-permute-start.3 = (f32[2,256,128]{2,1,0:T(8,128)S(1)}, f32[2,256,128]{2,1,0:T(8,128)S(1)}, u32[]{:S(2)}, u32[]{:S(2)}) collective-permute-start(f32[2,256,128]{2,1,0:T(8,128)S(1)} %pad_maximum_fusion.mine_ref), channel_id=1, source_target_pairs={{0,1},{1,0},{2,3},{3,2},{4,5},{5,4},{6,7},{7,6},{8,9},{9,8},{10,11... | collective-permute-start | bytes 786440 | tf_op jit(solution)/shard_map/ppermute | solution.py:222
  105.3 0.7 copy-start.4
  105.3 1.0 copy-start

commit v5 on v4

--- a/solution.py
+++ b/solution.py
@@ -56,13 +56,14 @@
     return upper, solved
 
 
-def factor_kernel(lead_ref, inv_ref, low_ref, work, upper):
+def factor_kernel(got_ref, inv_ref, low_ref, rows_ref, work, upper):
     eye = lax.broadcasted_iota(jnp.int32, (NB, NB), 0) == lax.broadcasted_iota(jnp.int32, (NB, NB), 1)
     eye = eye.astype(jnp.float32)
     zero = jnp.zeros((NB, NB), jnp.float32)
 
     def tile(core, n):
-        return lead_ref[core, :, n * PART : (n + 1) * PART, :].reshape(NB, NB)
+        starts = [(z * PANELS + n) * PART for z in range(NZ)]
+        return jnp.concatenate([got_ref[core, at : at + PART, :] for at in starts], axis=0)
 
     rows = ((tile(0, 0), tile(1, 0), tile(0, 1)), (tile(1, 1), tile(1, 2).T, zero), (tile(0, 2), zero, zero))
     for k, tiles in enumerate(rows):
@@ -104,22 +105,36 @@
 
     lax.fori_loop(0, PANELS, panel, 0)
 
-
-def factor(lead):
+    odd = lax.rem(lax.axis_index("col") // 2, 2)
+
+    def row_panel(core, near):
+        at = pl.multiple_of(NZ * PANELS * PART + near * 2 * NB, NB)
+        return got_ref[core, pl.ds(at, 2 * NB), :]
+
+    left = [row_panel(0, odd), row_panel(1, odd), row_panel(0, 1 - odd)]
+    rows0 = mm3_nt(left[0], inv_ref[0])
+    rows1 = mm3_nt(left[1] - mm3_nt(rows0, low_ref[0, 0]), inv_ref[1])
+    rows2 = mm3_nt(left[2] - mm3_nt(rows0, low_ref[0, 1]) - mm3_nt(rows1, low_ref[1, 0]), inv_ref[2])
+    for k, value in enumerate((rows0, rows1, rows2)):
+        rows_ref[:, k * NB : (k + 1) * NB] = value
+
+
+def factor(got):
     return pl.pallas_call(
         factor_kernel,
         out_shape=(
             jax.ShapeDtypeStruct((PANELS, NB, NB), jnp.float32),
             jax.ShapeDtypeStruct((PANELS - 1, 2, NB, NB), jnp.float32),
+            jax.ShapeDtypeStruct((2 * NB, PANELS * NB), jnp.float32),
         ),
         in_specs=[VMEM],
-        out_specs=[VMEM, VMEM],
+        out_specs=[VMEM] * 3,
         scratch_shapes=[
             pltpu.VMEM((PANELS + 1, NB, 4 * NB), jnp.float32),
             pltpu.VMEM((NB, 4 * NB), jnp.float32),
         ],
         name="factor",
-    )(lead)
+    )(got)
 
 
 def mm3_nt(a, b):
@@ -140,19 +155,12 @@
     )(got)
 
 
-def finish_kernel(inv_ref, low_ref, mine_ref, other_ref, y_ref, m_ref, out_ref, x_got):
+def finish_kernel(inv_ref, low_ref, rows_ref, y_ref, m_ref, out_ref):
     my_row = lax.axis_index("row")
     my_col = lax.axis_index("col")
     col_count = lax.axis_size("col")
     row_count = NX * NZ
-    core = lax.rem(my_col, 2)
-    odd = lax.rem(my_col // 2, 2)
-    x_got[core] = mine_ref[...]
-    x_got[1 - core] = other_ref[...]
-    left = [x_got[0, odd], x_got[1, odd], x_got[0, 1 - odd]]
-    rows0 = mm3_nt(left[0], inv_ref[0])
-    rows1 = mm3_nt(left[1] - mm3_nt(rows0, low_ref[0, 0]), inv_ref[1])
-    rows2 = mm3_nt(left[2] - mm3_nt(rows0, low_ref[0, 1]) - mm3_nt(rows1, low_ref[1, 0]), inv_ref[2])
+    rows = rows_ref[...]
     right = []
     for i in range(PANELS):
         tiles = []
@@ -163,9 +171,9 @@
     cols0 = mm3(inv_ref[0], right[0])
     cols1 = mm3(inv_ref[1], right[1] - mm3(low_ref[0, 0], cols0))
     cols2 = mm3(inv_ref[2], right[2] - mm3(low_ref[0, 1], cols0) - mm3(low_ref[1, 0], cols1))
-    rows = jnp.concatenate([rows0, rows1, rows2], axis=1)
     cols = jnp.concatenate([cols0, cols1, cols2], axis=0)
-    panel = jnp.where(my_col == 0, rows0, jnp.where(my_col == 1, rows1, rows2))
+    parts = [rows[:, k * NB : (k + 1) * NB] for k in range(PANELS)]
+    panel = jnp.where(my_col == 0, parts[0], jnp.where(my_col == 1, parts[1], parts[2]))
     u = lax.broadcasted_iota(jnp.int32, (NB, NB), 0)
     v = lax.broadcasted_iota(jnp.int32, (NB, NB), 1)
     for t in range(2):
@@ -182,15 +190,14 @@
             out_ref[t, pl.ds(s, NB, stride=4), :] = jnp.where(below + u >= v, value, 0.0)
 
 
-def finish(inverse, low, mine, other, y_part, matrix):
+def finish(inverse, low, rows, y_part, matrix):
     return pl.pallas_call(
         finish_kernel,
         out_shape=jax.ShapeDtypeStruct(matrix.shape, jnp.float32),
-        in_specs=[VMEM] * 6,
+        in_specs=[VMEM] * 5,
         out_specs=VMEM,
-        scratch_shapes=[pltpu.VMEM((2,) + mine.shape, jnp.float32)],
         name="finish",
-    )(inverse, low, mine, other, y_part, matrix)
+    )(inverse, low, rows, y_part, matrix)
 
 
 def to_all(value, axis, groups):
@@ -218,9 +225,6 @@
     for start in range(0, col_count, quarter):
         steps += [(start, start + 2), (start + 1, start + 3), (start + 2, start)]
     near = lax.ppermute(mine, "col", steps)
-    panels = jnp.stack([mine, near])
-    other = lax.ppermute(panels, "col", [(c, c ^ 1) for c in range(col_count)])
-
     piece = lax.all_to_all(matrix[0].reshape(NZ, PART * tile_cols, nb), "row", 0, 0, axis_index_groups=along_z)[0]
     head = piece.reshape(PART, tile_cols, nb)[:, 0, :]
     own = to_all(head, "col", along_y)[:2]
@@ -233,11 +237,12 @@
     ]
     lead = jnp.concatenate(lead, axis=0)
     lead = to_all(lead, "row", along_z)
-    lead = lax.all_gather(lead, "col", axis_index_groups=pairs)
+    sent = jnp.concatenate([lead.reshape(NZ * PANELS * PART, nb), mine, near], axis=0)
+    gathered = lax.all_gather(sent, "col", axis_index_groups=pairs)
     cols = pack(pack_cols_kernel, got, PANELS * PART * tile_cols)
     y_part = lax.all_to_all(cols, "row", 0, 0, axis_index_groups=along_z)
-    inverse, low = factor(lead)
-    out = finish(inverse, low, panels, other, y_part, matrix)
+    inverse, low, rows = factor(gathered)
+    out = finish(inverse, low, rows, y_part, matrix)
     return out.reshape(covariance.shape)
 
 

time: 112 us -> 110 us (0.982)
  starting transfers between devices: 27.5 us -> 13.6 us
  blocking collectives: 33.1 us -> 45.2 us
    ppermute x1 -> x0, starting transfers between devices: 14 us -> none  [per_device(): other = lax.ppermute(panels, 'col', [(c, c ^ 1) for c in range(col_count)])]
    all_gather x1, blocking collectives: 2.22 us -> 14.3 us  [per_device(): gathered = lax.all_gather(sent, 'col', axis_index_groups=pairs)]
    pallas_call x1, Pallas kernels: 12.5 us -> 13.7 us  [factor(): pl.pallas_call(factor_kernel, out_shape=(jax.ShapeDtypeStruct((PANELS, NB...]
  transfers between devices with their start and end apart: 7 -> 6, of which waited for: 3 -> 3; matrix products, arithmetic and copies ran while one was open for 0% -> 0% of each run, Pallas kernels for 13% -> 14%
where the time goes in v5:
time: 110 us
  blocking collectives  45.2 us (41%)
  waiting for transfers between devices  27.5 us (25%)
  Pallas kernels  19.7 us (18%)
  starting transfers between devices  13.6 us (12%)
  local copies, waits for them, and re-layouts  3.39 us (3%)
    all_to_all x1, blocking collectives, per_device(): lax.all_to_all(matrix[0].reshape(NZ, PART * tile_cols, nb), 'row', 0, 0,...  20.3 us
    ppermute x1, waiting for transfers between devices, per_device(): near = lax.ppermute(mine, 'col', steps)  15.7 us
    all_gather x1, blocking collectives, per_device(): gathered = lax.all_gather(sent, 'col', axis_index_groups=pairs)  14.3 us
    pallas_call x1, Pallas kernels, factor(): pl.pallas_call(factor_kernel, out_shape=(jax.ShapeDtypeStruct((PANELS, NB...  13.7 us
    all_to_all x2, waiting for transfers between devices, to_all(): lax.all_to_all(jnp.broadcast_to(value[None], (count,) + value.shape), axi...  11.8 us
    all_to_all x1, blocking collectives, to_all(): lax.all_to_all(jnp.broadcast_to(value[None], (count,) + value.shape), axi...  10.6 us
    all_to_all x2, starting transfers between devices, to_all(): lax.all_to_all(jnp.broadcast_to(value[None], (count,) + value.shape), axi...  7.41 us
    pallas_call x1, Pallas kernels, finish(): pl.pallas_call(finish_kernel, out_shape=jax.ShapeDtypeStruct(matrix.shape...  4.07 us
  transfers between devices with their start and end apart: 6, of which 3 were waited for; matrix products, arithmetic and copies ran while one was open for 0% of the time, Pallas kernels for 14%

profile of v5, /device:TPU:57, one launch (start us, length us, event | category | flops | bytes accessed | tf_op | source)
XLA Modules:
  0.0 109.6 jit_solution(13825420281269141768)
XLA Ops:
  0.0 0.0 slice-start
  0.0 0.9 slice-done
  1.0 20.3 %all_to_all.25 = f32[8,64,128]{2,1,0:T(8,128)S(1)} all-to-all(f32[8,64,128]{2,1,0:T(8,128)S(1)} %bitcast.19), channel_id=1, replica_groups={{0,64,128,192,256,320,384,448},{16,80,144,208,272,336,400,464},{32,96,1..., dimensions={0} | all-to-all | bytes 524288 | tf_op jit(solution)/shard_map/all_to_all | solution.py:228
  21.3 10.6 %all_to_all.26 = f32[8,16,128]{2,1,0:T(8,128)S(1)} all-to-all(f32[8,16,128]{2,1,0:T(8,128)S(1)} %broadcast_in_dim.9), channel_id=1, replica_groups={{0,2,4,6,8,10,12,14},{1,3,5,7,9,11,13,15},{16,18,20,22,24,26,28,30},{17..., dimensions={0} | all-to-all | bytes 131072 | tf_op jit(solution)/shard_map/all_to_all | solution.py:205
  31.9 0.7 broadcast_in_dim.10
  32.6 4.0 %all-to-all-start.2 = ((f32[4,96,128]{2,1,0:T(8,128)}), f32[4,96,128]{2,1,0:T(8,128)S(1)}, u32[]{:S(2)}, u32[]{:S(2)}) async-start(f32[4,96,128]{2,1,0:T(8,128)} %broadcast_in_dim.10), calls=%async_computation.2 | async-start | bytes 393216 | tf_op jit(solution)/shard_map/all_to_all | solution.py:205
  36.6 5.2 %all-to-all-done.2.got_ref = f32[4,96,128]{2,1,0:T(8,128)S(1)} async-done(((f32[4,96,128]{2,1,0:T(8,128)}), f32[4,96,128]{2,1,0:T(8,128)S(1)}, u32[]{:S(2)}, u32[]{:S(2)}) %all-to-all-start.2) | async-done | bytes 196640 | tf_op jit(solution)/shard_map/all_to_all | solution.py:205
  41.8 0.0 copy-start.2
  41.8 0.7 broadcast_in_dim.22
  42.5 0.0 copy-done.2
  42.5 3.4 %all-to-all-start.3 = ((f32[8,48,128]{2,1,0:T(8,128)}), f32[8,48,128]{2,1,0:T(8,128)S(1)}, u32[]{:S(2)}, u32[]{:S(2)}) async-start(f32[8,48,128]{2,1,0:T(8,128)} %broadcast_in_dim.22), calls=%async_computation.3 | async-start | bytes 393216 | tf_op jit(solution)/shard_map/all_to_all | solution.py:205
  45.9 1.9 %shard_map.17 = f32[8,192,128]{2,1,0:T(8,128)} custom-call(f32[4,96,128]{2,1,0:T(8,128)} %copy-done.2), custom_call_target="tpu_custom_call" | custom-call | tf_op jit(solution)/shard_map/pallas_call | solution.py:153
  47.8 0.0 copy-start.1
  47.8 6.6 %all-to-all-done.3 = f32[8,48,128]{2,1,0:T(8,128)S(1)} async-done(((f32[8,48,128]{2,1,0:T(8,128)}), f32[8,48,128]{2,1,0:T(8,128)S(1)}, u32[]{:S(2)}, u32[]{:S(2)}) %all-to-all-start.3) | async-done | bytes 196640 | tf_op jit(solution)/shard_map/all_to_all | solution.py:205
  54.5 3.5 %all-to-all-start.4 = ((f32[8,192,128]{2,1,0:T(8,128)}), f32[8,192,128]{2,1,0:T(8,128)S(1)}, u32[]{:S(2)}, u32[]{:S(2)}) async-start(f32[8,192,128]{2,1,0:T(8,128)} %shard_map.17), calls=%async_computation.4 | async-start | bytes 1572864 | tf_op jit(solution)/shard_map/all_to_all | solution.py:243
  58.0 0.0 copy-done.1
  58.0 0.1 slice.40
  58.1 0.7 collective-permute-start
  58.8 0.0 collective-permute-done
  58.9 0.7 collective-permute-start.1
  59.5 0.0 collective-permute-done.1
  59.6 1.3 %collective-permute-start.2 = (f32[256,128]{1,0:T(8,128)S(1)}, f32[256,128]{1,0:T(8,128)S(1)}, u32[]{:S(2)}, u32[]{:S(2)}) collective-permute-start(f32[256,128]{1,0:T(8,128)S(1)} %broadcast_select_fusion.1), channel_id=1, source_target_pairs={{0,2},{1,3},{2,0},{4,6},{5,7},{6,4},{8,10},{9,11},{10,8},{12,14},{... | collective-permute-start | bytes 393224 | tf_op jit(solution)/shard_map/ppermute | solution.py:227
  60.9 15.7 %collective-permute-done.2 = f32[256,128]{1,0:T(8,128)S(1)} collective-permute-done((f32[256,128]{1,0:T(8,128)S(1)}, f32[256,128]{1,0:T(8,128)S(1)}, u32[]{:S(2)}, u32[]{:S(2)}) %collective-permute-start.2) | collective-permute-done | bytes 131104 | tf_op jit(solution)/shard_map/ppermute | solution.py:227
  76.6 14.3 %all-gather = f32[1792,128]{1,0:T(8,128)} all-gather(f32[896,128]{1,0:T(8,128)S(1)} %pad_maximum_fusion), channel_id=2, replica_groups={{0,1},{2,3},{4,5},{6,7},{8,9},{10,11},{12,13},{14,15},{16,17},{18,19},{..., dimensions={0}, use_global_device_ids=true | all-gather | bytes 1376256 | tf_op jit(solution)/shard_map/all_gather | solution.py:241
  90.9 13.7 %factor.1 = (f32[3,128,128]{2,1,0:T(8,128)}, f32[2,2,128,128]{3,2,1,0:T(8,128)}, f32[256,384]{1,0:T(8,128)}) custom-call(f32[2,896,128]{2,1,0:T(8,128)} %bitcast.17), custom_call_target="tpu_custom_call" | custom-call | tf_op jit(solution)/shard_map/factor/pallas_call | solution.py:123
  104.6 0.0 all-to-all-done.4.y_ref
  104.6 0.0 copy-start
  104.6 0.9 copy-done
  105.5 4.1 %finish.1 = f32[2,512,128]{2,1,0:T(8,128)} custom-call(f32[3,128,128]{2,1,0:T(8,128)} %get-tuple-element.8.inv_ref, f32[2,2,128,128]{3,2,1,0:T(8,128)} %get-tuple-element.9.low_ref, f32[256,384]{1,0:T(8,128)} %get-tuple-element.10.rows_ref, f32[8,192,128]{2,1,0:T(8,128)} %copy-done, f32[2,512,128]{2,1,0:T(8,128)} %bitcast.18), custom_call_target="tpu_custom_call" | custom-call | tf_op jit(solution)/shard_map/finish/pallas_call | solution.py:194
  (10 shorter events, 0.1 us)
Async XLA Ops:
  0.0 0.9 slice-start
  32.6 9.2 %all-to-all-start.2 = ((f32[4,96,128]{2,1,0:T(8,128)}), f32[4,96,128]{2,1,0:T(8,128)S(1)}, u32[]{:S(2)}, u32[]{:S(2)}) async-start(f32[4,96,128]{2,1,0:T(8,128)} %broadcast_in_dim.10), calls=%async_computation.2 | async-start | bytes 393216 | tf_op jit(solution)/shard_map/all_to_all | solution.py:205
  41.8 0.7 copy-start.2
  42.5 11.9 %all-to-all-start.3 = ((f32[8,48,128]{2,1,0:T(8,128)}), f32[8,48,128]{2,1,0:T(8,128)S(1)}, u32[]{:S(2)}, u32[]{:S(2)}) async-start(f32[8,48,128]{2,1,0:T(8,128)} %broadcast_in_dim.22), calls=%async_computation.3 | async-start | bytes 393216 | tf_op jit(solution)/shard_map/all_to_all | solution.py:205
  47.8 10.2 %copy-start.1 = (f32[2,128,4,128]{3,2,1,0:T(4,128)S(1)}, f32[2,128,4,128]{3,2,1,0:T(4,128)}, u32[]{:S(2)}) copy-start(f32[2,128,4,128]{3,2,1,0:T(4,128)} %param.1) | copy-start | bytes 1572868
  54.5 50.1 %all-to-all-start.4 = ((f32[8,192,128]{2,1,0:T(8,128)}), f32[8,192,128]{2,1,0:T(8,128)S(1)}, u32[]{:S(2)}, u32[]{:S(2)}) async-start(f32[8,192,128]{2,1,0:T(8,128)} %shard_map.17), calls=%async_computation.4 | async-start | bytes 1572864 | tf_op jit(solution)/shard_map/all_to_all | solution.py:243
  58.1 0.7 collective-permute-start
  58.9 0.7 collective-permute-start.1
  59.6 17.0 %collective-permute-start.2 = (f32[256,128]{1,0:T(8,128)S(1)}, f32[256,128]{1,0:T(8,128)S(1)}, u32[]{:S(2)}, u32[]{:S(2)}) collective-permute-start(f32[256,128]{1,0:T(8,128)S(1)} %broadcast_select_fusion.1), channel_id=1, source_target_pairs={{0,2},{1,3},{2,0},{4,6},{5,7},{6,4},{8,10},{9,11},{10,8},{12,14},{... | collective-permute-start | bytes 393224 | tf_op jit(solution)/shard_map/ppermute | solution.py:227
  104.6 0.9 copy-start

commit v6 on v5

--- a/solution.py
+++ b/solution.py
@@ -14,10 +14,6 @@
 PART = NB // NZ
 VMEM = pl.BlockSpec(memory_space=pltpu.VMEM)
 SMEM = pl.BlockSpec(memory_space=pltpu.SMEM)
-
-
-def mm(a, b):
-    return jnp.dot(a, b, precision=lax.Precision.HIGHEST, preferred_element_type=jnp.float32)
 
 
 def mm3(a, b, contract=(1, 0)):
@@ -56,7 +52,7 @@
     return upper, solved
 
 
-def factor_kernel(got_ref, inv_ref, low_ref, rows_ref, work, upper):
+def factor_kernel(got_ref, panel_ref, gain_ref, inv_ref, low_ref, work, upper):
     eye = lax.broadcasted_iota(jnp.int32, (NB, NB), 0) == lax.broadcasted_iota(jnp.int32, (NB, NB), 1)
     eye = eye.astype(jnp.float32)
     zero = jnp.zeros((NB, NB), jnp.float32)
@@ -97,9 +93,9 @@
             l2 = u2.T
             low_ref[k, 0] = l1
             low_ref[k, 1] = l2
-            work[k + 1, :, :NB] -= mm(l1, u1)
-            work[k + 1, :, 2 * NB : 3 * NB] -= mm(l1, u2)
-            work[k + 2, :, :NB] -= mm(l2, u2)
+            work[k + 1, :, :NB] -= mm3(l1, u1)
+            work[k + 1, :, 2 * NB : 3 * NB] -= mm3(l1, u2)
+            work[k + 2, :, :NB] -= mm3(l2, u2)
 
         return carry
 
@@ -115,21 +111,27 @@
     rows0 = mm3_nt(left[0], inv_ref[0])
     rows1 = mm3_nt(left[1] - mm3_nt(rows0, low_ref[0, 0]), inv_ref[1])
     rows2 = mm3_nt(left[2] - mm3_nt(rows0, low_ref[0, 1]) - mm3_nt(rows1, low_ref[1, 0]), inv_ref[2])
-    for k, value in enumerate((rows0, rows1, rows2)):
-        rows_ref[:, k * NB : (k + 1) * NB] = value
+    my_col = lax.axis_index("col")
+    panel_ref[...] = jnp.where(my_col == 0, rows0, jnp.where(my_col == 1, rows1, rows2))
+    gain2 = mm3(rows2, inv_ref[2])
+    gain1 = mm3(rows1 - mm3(gain2, low_ref[1, 0]), inv_ref[1])
+    gain0 = mm3(rows0 - mm3(gain1, low_ref[0, 0]) - mm3(gain2, low_ref[0, 1]), inv_ref[0])
+    for k, value in enumerate((gain0, gain1, gain2)):
+        gain_ref[:, k * NB : (k + 1) * NB] = value
 
 
 def factor(got):
     return pl.pallas_call(
         factor_kernel,
         out_shape=(
-            jax.ShapeDtypeStruct((PANELS, NB, NB), jnp.float32),
-            jax.ShapeDtypeStruct((PANELS - 1, 2, NB, NB), jnp.float32),
+            jax.ShapeDtypeStruct((2 * NB, NB), jnp.float32),
             jax.ShapeDtypeStruct((2 * NB, PANELS * NB), jnp.float32),
         ),
         in_specs=[VMEM],
-        out_specs=[VMEM] * 3,
+        out_specs=[VMEM] * 2,
         scratch_shapes=[
+            pltpu.VMEM((PANELS, NB, NB), jnp.float32),
+            pltpu.VMEM((PANELS - 1, 2, NB, NB), jnp.float32),
             pltpu.VMEM((PANELS + 1, NB, 4 * NB), jnp.float32),
             pltpu.VMEM((NB, 4 * NB), jnp.float32),
         ],
@@ -155,12 +157,12 @@
     )(got)
 
 
-def finish_kernel(inv_ref, low_ref, rows_ref, y_ref, m_ref, out_ref):
+def finish_kernel(panel_ref, gain_ref, y_ref, m_ref, out_ref):
     my_row = lax.axis_index("row")
     my_col = lax.axis_index("col")
     col_count = lax.axis_size("col")
     row_count = NX * NZ
-    rows = rows_ref[...]
+    gain = gain_ref[...]
     right = []
     for i in range(PANELS):
         tiles = []
@@ -168,36 +170,31 @@
             at = i * PART * 4 + s
             tiles.append(jnp.concatenate([y_ref[z, pl.ds(at, PART, stride=4), :] for z in range(NZ)], axis=0))
         right.append(jnp.concatenate(tiles, axis=1))
-    cols0 = mm3(inv_ref[0], right[0])
-    cols1 = mm3(inv_ref[1], right[1] - mm3(low_ref[0, 0], cols0))
-    cols2 = mm3(inv_ref[2], right[2] - mm3(low_ref[0, 1], cols0) - mm3(low_ref[1, 0], cols1))
-    cols = jnp.concatenate([cols0, cols1, cols2], axis=0)
-    parts = [rows[:, k * NB : (k + 1) * NB] for k in range(PANELS)]
-    panel = jnp.where(my_col == 0, parts[0], jnp.where(my_col == 1, parts[1], parts[2]))
+    cols = jnp.concatenate(right, axis=0)
     u = lax.broadcasted_iota(jnp.int32, (NB, NB), 0)
     v = lax.broadcasted_iota(jnp.int32, (NB, NB), 1)
     for t in range(2):
         live = min(4, -(-(t + 1) * row_count // col_count))
-        product = mm3(rows[t * NB : (t + 1) * NB], cols[:, : live * NB])
+        product = mm3(gain[t * NB : (t + 1) * NB], cols[:, : live * NB])
         for s in range(4):
             if s >= live:
                 out_ref[t, pl.ds(s, NB, stride=4), :] = jnp.zeros((NB, NB), jnp.float32)
                 continue
             value = m_ref[t, pl.ds(s, NB, stride=4), :] - product[:, s * NB : (s + 1) * NB]
             if s == 0:
-                value = jnp.where(my_col < PANELS, panel[t * NB : (t + 1) * NB], value)
+                value = jnp.where(my_col < PANELS, panel_ref[t * NB : (t + 1) * NB, :], value)
             below = (t * row_count + my_row - s * col_count - my_col) * NB
             out_ref[t, pl.ds(s, NB, stride=4), :] = jnp.where(below + u >= v, value, 0.0)
 
 
-def finish(inverse, low, rows, y_part, matrix):
+def finish(panel, gain, y_part, matrix):
     return pl.pallas_call(
         finish_kernel,
         out_shape=jax.ShapeDtypeStruct(matrix.shape, jnp.float32),
-        in_specs=[VMEM] * 5,
+        in_specs=[VMEM] * 4,
         out_specs=VMEM,
         name="finish",
-    )(inverse, low, rows, y_part, matrix)
+    )(panel, gain, y_part, matrix)
 
 
 def to_all(value, axis, groups):
@@ -241,8 +238,8 @@
     gathered = lax.all_gather(sent, "col", axis_index_groups=pairs)
     cols = pack(pack_cols_kernel, got, PANELS * PART * tile_cols)
     y_part = lax.all_to_all(cols, "row", 0, 0, axis_index_groups=along_z)
-    inverse, low, rows = factor(gathered)
-    out = finish(inverse, low, rows, y_part, matrix)
+    panel, gain = factor(gathered)
+    out = finish(panel, gain, y_part, matrix)
     return out.reshape(covariance.shape)
 
 

time: 110 us -> 110 us (level)
    pallas_call x1, Pallas kernels: 4.07 us -> 2.72 us  [finish(): pl.pallas_call(finish_kernel, out_shape=jax.ShapeDtypeStruct(matrix.shape...]
  transfers between devices with their start and end apart: 6 -> 6, of which waited for: 3 -> 3; matrix products, arithmetic and copies ran while one was open for 0% -> 0% of each run, Pallas kernels for 14% -> 15%
where the time goes in v6:
time: 110 us; the launch traced here: 109 us
  blocking collectives  45.2 us (41%)
  waiting for transfers between devices  27.5 us (25%)
  Pallas kernels  19.1 us (17%)
  starting transfers between devices  13.6 us (12%)
  local copies, waits for them, and re-layouts  3.39 us (3%)
    all_to_all x1, blocking collectives, per_device(): lax.all_to_all(matrix[0].reshape(NZ, PART * tile_cols, nb), 'row', 0, 0,...  20.3 us
    ppermute x1, waiting for transfers between devices, per_device(): near = lax.ppermute(mine, 'col', steps)  15.7 us
    pallas_call x1, Pallas kernels, factor(): pl.pallas_call(factor_kernel, out_shape=(jax.ShapeDtypeStruct((2 * NB, NB...  14.5 us
    all_gather x1, blocking collectives, per_device(): gathered = lax.all_gather(sent, 'col', axis_index_groups=pairs)  14.3 us
    all_to_all x2, waiting for transfers between devices, to_all(): lax.all_to_all(jnp.broadcast_to(value[None], (count,) + value.shape), axi...  11.8 us
    all_to_all x1, blocking collectives, to_all(): lax.all_to_all(jnp.broadcast_to(value[None], (count,) + value.shape), axi...  10.6 us
    all_to_all x2, starting transfers between devices, to_all(): lax.all_to_all(jnp.broadcast_to(value[None], (count,) + value.shape), axi...  7.41 us
    all_to_all x1, starting transfers between devices, per_device(): y_part = lax.all_to_all(cols, 'row', 0, 0, axis_index_groups=along_z)  3.55 us
  transfers between devices with their start and end apart: 6, of which 3 were waited for; matrix products, arithmetic and copies ran while one was open for 0% of the time, Pallas kernels for 15%

profile of v6, /device:TPU:57, one launch (start us, length us, event | category | flops | bytes accessed | tf_op | source)
XLA Modules:
  0.0 109.0 jit_solution(13792795394495233255)
XLA Ops:
  0.0 0.0 slice-start
  0.0 0.9 slice-done
  1.0 20.3 %all_to_all.25 = f32[8,64,128]{2,1,0:T(8,128)S(1)} all-to-all(f32[8,64,128]{2,1,0:T(8,128)S(1)} %bitcast.19), channel_id=1, replica_groups={{0,64,128,192,256,320,384,448},{16,80,144,208,272,336,400,464},{32,96,1..., dimensions={0} | all-to-all | bytes 524288 | tf_op jit(solution)/shard_map/all_to_all | solution.py:225
  21.3 10.6 %all_to_all.26 = f32[8,16,128]{2,1,0:T(8,128)S(1)} all-to-all(f32[8,16,128]{2,1,0:T(8,128)S(1)} %broadcast_in_dim.9), channel_id=1, replica_groups={{0,2,4,6,8,10,12,14},{1,3,5,7,9,11,13,15},{16,18,20,22,24,26,28,30},{17..., dimensions={0} | all-to-all | bytes 131072 | tf_op jit(solution)/shard_map/all_to_all | solution.py:202
  31.9 0.7 broadcast_in_dim.10
  32.6 4.0 %all-to-all-start.2 = ((f32[4,96,128]{2,1,0:T(8,128)}), f32[4,96,128]{2,1,0:T(8,128)S(1)}, u32[]{:S(2)}, u32[]{:S(2)}) async-start(f32[4,96,128]{2,1,0:T(8,128)} %broadcast_in_dim.10), calls=%async_computation.2 | async-start | bytes 393216 | tf_op jit(solution)/shard_map/all_to_all | solution.py:202
  36.6 5.2 %all-to-all-done.2.got_ref = f32[4,96,128]{2,1,0:T(8,128)S(1)} async-done(((f32[4,96,128]{2,1,0:T(8,128)}), f32[4,96,128]{2,1,0:T(8,128)S(1)}, u32[]{:S(2)}, u32[]{:S(2)}) %all-to-all-start.2) | async-done | bytes 196640 | tf_op jit(solution)/shard_map/all_to_all | solution.py:202
  41.8 0.0 copy-start.2
  41.8 0.7 broadcast_in_dim.22
  42.5 0.0 copy-done.2
  42.5 3.4 %all-to-all-start.3 = ((f32[8,48,128]{2,1,0:T(8,128)}), f32[8,48,128]{2,1,0:T(8,128)S(1)}, u32[]{:S(2)}, u32[]{:S(2)}) async-start(f32[8,48,128]{2,1,0:T(8,128)} %broadcast_in_dim.22), calls=%async_computation.3 | async-start | bytes 393216 | tf_op jit(solution)/shard_map/all_to_all | solution.py:202
  45.9 1.9 %shard_map.17 = f32[8,192,128]{2,1,0:T(8,128)} custom-call(f32[4,96,128]{2,1,0:T(8,128)} %copy-done.2), custom_call_target="tpu_custom_call" | custom-call | tf_op jit(solution)/shard_map/pallas_call | solution.py:155
  47.8 0.0 copy-start.1
  47.8 6.6 %all-to-all-done.3 = f32[8,48,128]{2,1,0:T(8,128)S(1)} async-done(((f32[8,48,128]{2,1,0:T(8,128)}), f32[8,48,128]{2,1,0:T(8,128)S(1)}, u32[]{:S(2)}, u32[]{:S(2)}) %all-to-all-start.3) | async-done | bytes 196640 | tf_op jit(solution)/shard_map/all_to_all | solution.py:202
  54.5 3.5 %all-to-all-start.4 = ((f32[8,192,128]{2,1,0:T(8,128)}), f32[8,192,128]{2,1,0:T(8,128)S(1)}, u32[]{:S(2)}, u32[]{:S(2)}) async-start(f32[8,192,128]{2,1,0:T(8,128)} %shard_map.17), calls=%async_computation.4 | async-start | bytes 1572864 | tf_op jit(solution)/shard_map/all_to_all | solution.py:240
  58.0 0.0 copy-done.1
  58.0 0.1 slice.40
  58.1 0.7 collective-permute-start
  58.8 0.0 collective-permute-done
  58.9 0.7 collective-permute-start.1
  59.5 0.0 collective-permute-done.1
  59.6 1.3 %collective-permute-start.2 = (f32[256,128]{1,0:T(8,128)S(1)}, f32[256,128]{1,0:T(8,128)S(1)}, u32[]{:S(2)}, u32[]{:S(2)}) collective-permute-start(f32[256,128]{1,0:T(8,128)S(1)} %broadcast_select_fusion.1), channel_id=1, source_target_pairs={{0,2},{1,3},{2,0},{4,6},{5,7},{6,4},{8,10},{9,11},{10,8},{12,14},{... | collective-permute-start | bytes 393224 | tf_op jit(solution)/shard_map/ppermute | solution.py:224
  60.9 15.7 %collective-permute-done.2 = f32[256,128]{1,0:T(8,128)S(1)} collective-permute-done((f32[256,128]{1,0:T(8,128)S(1)}, f32[256,128]{1,0:T(8,128)S(1)}, u32[]{:S(2)}, u32[]{:S(2)}) %collective-permute-start.2) | collective-permute-done | bytes 131104 | tf_op jit(solution)/shard_map/ppermute | solution.py:224
  76.6 14.3 %all-gather = f32[1792,128]{1,0:T(8,128)} all-gather(f32[896,128]{1,0:T(8,128)S(1)} %pad_maximum_fusion), channel_id=2, replica_groups={{0,1},{2,3},{4,5},{6,7},{8,9},{10,11},{12,13},{14,15},{16,17},{18,19},{..., dimensions={0}, use_global_device_ids=true | all-gather | bytes 1376256 | tf_op jit(solution)/shard_map/all_gather | solution.py:238
  90.9 14.5 %factor.1 = (f32[256,128]{1,0:T(8,128)}, f32[256,384]{1,0:T(8,128)}) custom-call(f32[2,896,128]{2,1,0:T(8,128)} %bitcast.17), custom_call_target="tpu_custom_call" | custom-call | tf_op jit(solution)/shard_map/factor/pallas_call | solution.py:124
  105.4 0.0 all-to-all-done.4.y_ref
  105.4 0.0 copy-start
  105.4 0.9 copy-done
  106.3 2.7 %finish.1 = f32[2,512,128]{2,1,0:T(8,128)} custom-call(f32[256,128]{1,0:T(8,128)} %get-tuple-element.7.panel_ref, f32[256,384]{1,0:T(8,128)} %get-tuple-element.8.gain_ref, f32[8,192,128]{2,1,0:T(8,128)} %copy-done, f32[2,512,128]{2,1,0:T(8,128)} %bitcast.18), custom_call_target="tpu_custom_call" | custom-call | tf_op jit(solution)/shard_map/finish/pallas_call | solution.py:191
  (10 shorter events, 0.1 us)
Async XLA Ops:
  0.0 0.9 slice-start
  32.6 9.2 %all-to-all-start.2 = ((f32[4,96,128]{2,1,0:T(8,128)}), f32[4,96,128]{2,1,0:T(8,128)S(1)}, u32[]{:S(2)}, u32[]{:S(2)}) async-start(f32[4,96,128]{2,1,0:T(8,128)} %broadcast_in_dim.10), calls=%async_computation.2 | async-start | bytes 393216 | tf_op jit(solution)/shard_map/all_to_all | solution.py:202
  41.8 0.7 copy-start.2
  42.5 11.9 %all-to-all-start.3 = ((f32[8,48,128]{2,1,0:T(8,128)}), f32[8,48,128]{2,1,0:T(8,128)S(1)}, u32[]{:S(2)}, u32[]{:S(2)}) async-start(f32[8,48,128]{2,1,0:T(8,128)} %broadcast_in_dim.22), calls=%async_computation.3 | async-start | bytes 393216 | tf_op jit(solution)/shard_map/all_to_all | solution.py:202
  47.8 10.2 %copy-start.1 = (f32[2,128,4,128]{3,2,1,0:T(4,128)S(1)}, f32[2,128,4,128]{3,2,1,0:T(4,128)}, u32[]{:S(2)}) copy-start(f32[2,128,4,128]{3,2,1,0:T(4,128)} %param.1) | copy-start | bytes 1572868
  54.5 50.9 %all-to-all-start.4 = ((f32[8,192,128]{2,1,0:T(8,128)}), f32[8,192,128]{2,1,0:T(8,128)S(1)}, u32[]{:S(2)}, u32[]{:S(2)}) async-start(f32[8,192,128]{2,1,0:T(8,128)} %shard_map.17), calls=%async_computation.4 | async-start | bytes 1572864 | tf_op jit(solution)/shard_map/all_to_all | solution.py:240
  58.1 0.7 collective-permute-start
  58.9 0.7 collective-permute-start.1
  59.6 17.0 %collective-permute-start.2 = (f32[256,128]{1,0:T(8,128)S(1)}, f32[256,128]{1,0:T(8,128)S(1)}, u32[]{:S(2)}, u32[]{:S(2)}) collective-permute-start(f32[256,128]{1,0:T(8,128)S(1)} %broadcast_select_fusion.1), channel_id=1, source_target_pairs={{0,2},{1,3},{2,0},{4,6},{5,7},{6,4},{8,10},{9,11},{10,8},{12,14},{... | collective-permute-start | bytes 393224 | tf_op jit(solution)/shard_map/ppermute | solution.py:224
  105.4 0.9 copy-start

commit v7 on v6

--- a/solution.py
+++ b/solution.py
@@ -67,7 +67,15 @@
             work[k, :, q * NB : (q + 1) * NB] = value
         work[k, :, NB : 2 * NB] = eye
 
-    def panel(k, carry):
+    odd = lax.rem(lax.axis_index("col") // 2, 2)
+
+    def row_panel(core, near):
+        at = pl.multiple_of(NZ * PANELS * PART + near * 2 * NB, NB)
+        return got_ref[core, pl.ds(at, 2 * NB), :]
+
+    left = [row_panel(0, odd), row_panel(1, odd), row_panel(0, 1 - odd)]
+    rows = []
+    for k in range(PANELS):
         strip = work[k, 0:STRIP, :]
         for b in range(NB // STRIP):
             first = b * STRIP
@@ -85,8 +93,11 @@
                     work[k, first + 2 * STRIP :, :] = below - mm3(below[:, :NB], padded)
         inv_ref[k] = upper[:, NB : 2 * NB]
 
-        @pl.when(k < PANELS - 1)
-        def _():
+        mine = left[k]
+        for j in range(k):
+            mine = mine - mm3_nt(rows[j], low_ref[j, k - j - 1])
+        rows.append(mm3_nt(mine, inv_ref[k]))
+        if k < PANELS - 1:
             u1 = upper[:, 2 * NB : 3 * NB]
             u2 = upper[:, 3 * NB :]
             l1 = u1.T
@@ -96,21 +107,7 @@
             work[k + 1, :, :NB] -= mm3(l1, u1)
             work[k + 1, :, 2 * NB : 3 * NB] -= mm3(l1, u2)
             work[k + 2, :, :NB] -= mm3(l2, u2)
-
-        return carry
-
-    lax.fori_loop(0, PANELS, panel, 0)
-
-    odd = lax.rem(lax.axis_index("col") // 2, 2)
-
-    def row_panel(core, near):
-        at = pl.multiple_of(NZ * PANELS * PART + near * 2 * NB, NB)
-        return got_ref[core, pl.ds(at, 2 * NB), :]
-
-    left = [row_panel(0, odd), row_panel(1, odd), row_panel(0, 1 - odd)]
-    rows0 = mm3_nt(left[0], inv_ref[0])
-    rows1 = mm3_nt(left[1] - mm3_nt(rows0, low_ref[0, 0]), inv_ref[1])
-    rows2 = mm3_nt(left[2] - mm3_nt(rows0, low_ref[0, 1]) - mm3_nt(rows1, low_ref[1, 0]), inv_ref[2])
+    rows0, rows1, rows2 = rows
     my_col = lax.axis_index("col")
     panel_ref[...] = jnp.where(my_col == 0, rows0, jnp.where(my_col == 1, rows1, rows2))
     gain2 = mm3(rows2, inv_ref[2])

time: 110 us -> 109 us (level)
  transfers between devices with their start and end apart: 6 -> 6, of which waited for: 3 -> 3; matrix products, arithmetic and copies ran while one was open for 0% -> 0% of each run, Pallas kernels for 15% -> 14%
where the time goes in v7:
time: 109 us; the launch traced here: 108 us
  blocking collectives  45.2 us (41%)
  waiting for transfers between devices  27.5 us (25%)
  Pallas kernels  18.2 us (17%)
  starting transfers between devices  13.6 us (12%)
  local copies, waits for them, and re-layouts  3.39 us (3%)
    all_to_all x1, blocking collectives, per_device(): lax.all_to_all(matrix[0].reshape(NZ, PART * tile_cols, nb), 'row', 0, 0,...  20.3 us
    ppermute x1, waiting for transfers between devices, per_device(): near = lax.ppermute(mine, 'col', steps)  15.7 us
    all_gather x1, blocking collectives, per_device(): gathered = lax.all_gather(sent, 'col', axis_index_groups=pairs)  14.3 us
    pallas_call x1, Pallas kernels, factor(): pl.pallas_call(factor_kernel, out_shape=(jax.ShapeDtypeStruct((2 * NB, NB...  13.6 us
    all_to_all x2, waiting for transfers between devices, to_all(): lax.all_to_all(jnp.broadcast_to(value[None], (count,) + value.shape), axi...  11.8 us
    all_to_all x1, blocking collectives, to_all(): lax.all_to_all(jnp.broadcast_to(value[None], (count,) + value.shape), axi...  10.6 us
    all_to_all x2, starting transfers between devices, to_all(): lax.all_to_all(jnp.broadcast_to(value[None], (count,) + value.shape), axi...  7.41 us
    all_to_all x1, starting transfers between devices, per_device(): y_part = lax.all_to_all(cols, 'row', 0, 0, axis_index_groups=along_z)  3.55 us
  transfers between devices with their start and end apart: 6, of which 3 were waited for; matrix products, arithmetic and copies ran while one was open for 0% of the time, Pallas kernels for 14%

profile of v7, /device:TPU:57, one launch (start us, length us, event | category | flops | bytes accessed | tf_op | source)
XLA Modules:
  0.0 108.1 jit_solution(13605539118932430187)
XLA Ops:
  0.0 0.0 slice-start
  0.0 0.9 slice-done
  1.0 20.3 %all_to_all.25 = f32[8,64,128]{2,1,0:T(8,128)S(1)} all-to-all(f32[8,64,128]{2,1,0:T(8,128)S(1)} %bitcast.19), channel_id=1, replica_groups={{0,64,128,192,256,320,384,448},{16,80,144,208,272,336,400,464},{32,96,1..., dimensions={0} | all-to-all | bytes 524288 | tf_op jit(solution)/shard_map/all_to_all | solution.py:222
  21.3 10.6 %all_to_all.26 = f32[8,16,128]{2,1,0:T(8,128)S(1)} all-to-all(f32[8,16,128]{2,1,0:T(8,128)S(1)} %broadcast_in_dim.9), channel_id=1, replica_groups={{0,2,4,6,8,10,12,14},{1,3,5,7,9,11,13,15},{16,18,20,22,24,26,28,30},{17..., dimensions={0} | all-to-all | bytes 131072 | tf_op jit(solution)/shard_map/all_to_all | solution.py:199
  31.9 0.7 broadcast_in_dim.10
  32.6 4.0 %all-to-all-start.2 = ((f32[4,96,128]{2,1,0:T(8,128)}), f32[4,96,128]{2,1,0:T(8,128)S(1)}, u32[]{:S(2)}, u32[]{:S(2)}) async-start(f32[4,96,128]{2,1,0:T(8,128)} %broadcast_in_dim.10), calls=%async_computation.2 | async-start | bytes 393216 | tf_op jit(solution)/shard_map/all_to_all | solution.py:199
  36.6 5.2 %all-to-all-done.2.got_ref = f32[4,96,128]{2,1,0:T(8,128)S(1)} async-done(((f32[4,96,128]{2,1,0:T(8,128)}), f32[4,96,128]{2,1,0:T(8,128)S(1)}, u32[]{:S(2)}, u32[]{:S(2)}) %all-to-all-start.2) | async-done | bytes 196640 | tf_op jit(solution)/shard_map/all_to_all | solution.py:199
  41.8 0.0 copy-start.2
  41.8 0.7 broadcast_in_dim.22
  42.5 0.0 copy-done.2
  42.5 3.4 %all-to-all-start.3 = ((f32[8,48,128]{2,1,0:T(8,128)}), f32[8,48,128]{2,1,0:T(8,128)S(1)}, u32[]{:S(2)}, u32[]{:S(2)}) async-start(f32[8,48,128]{2,1,0:T(8,128)} %broadcast_in_dim.22), calls=%async_computation.3 | async-start | bytes 393216 | tf_op jit(solution)/shard_map/all_to_all | solution.py:199
  45.9 1.9 %shard_map.17 = f32[8,192,128]{2,1,0:T(8,128)} custom-call(f32[4,96,128]{2,1,0:T(8,128)} %copy-done.2), custom_call_target="tpu_custom_call" | custom-call | tf_op jit(solution)/shard_map/pallas_call | solution.py:152
  47.8 0.0 copy-start.1
  47.8 6.6 %all-to-all-done.3 = f32[8,48,128]{2,1,0:T(8,128)S(1)} async-done(((f32[8,48,128]{2,1,0:T(8,128)}), f32[8,48,128]{2,1,0:T(8,128)S(1)}, u32[]{:S(2)}, u32[]{:S(2)}) %all-to-all-start.3) | async-done | bytes 196640 | tf_op jit(solution)/shard_map/all_to_all | solution.py:199
  54.5 3.5 %all-to-all-start.4 = ((f32[8,192,128]{2,1,0:T(8,128)}), f32[8,192,128]{2,1,0:T(8,128)S(1)}, u32[]{:S(2)}, u32[]{:S(2)}) async-start(f32[8,192,128]{2,1,0:T(8,128)} %shard_map.17), calls=%async_computation.4 | async-start | bytes 1572864 | tf_op jit(solution)/shard_map/all_to_all | solution.py:237
  58.0 0.0 copy-done.1
  58.0 0.1 slice.40
  58.1 0.7 collective-permute-start
  58.8 0.0 collective-permute-done
  58.9 0.7 collective-permute-start.1
  59.5 0.0 collective-permute-done.1
  59.6 1.3 %collective-permute-start.2 = (f32[256,128]{1,0:T(8,128)S(1)}, f32[256,128]{1,0:T(8,128)S(1)}, u32[]{:S(2)}, u32[]{:S(2)}) collective-permute-start(f32[256,128]{1,0:T(8,128)S(1)} %broadcast_select_fusion.1), channel_id=1, source_target_pairs={{0,2},{1,3},{2,0},{4,6},{5,7},{6,4},{8,10},{9,11},{10,8},{12,14},{... | collective-permute-start | bytes 393224 | tf_op jit(solution)/shard_map/ppermute | solution.py:221
  60.9 15.7 %collective-permute-done.2 = f32[256,128]{1,0:T(8,128)S(1)} collective-permute-done((f32[256,128]{1,0:T(8,128)S(1)}, f32[256,128]{1,0:T(8,128)S(1)}, u32[]{:S(2)}, u32[]{:S(2)}) %collective-permute-start.2) | collective-permute-done | bytes 131104 | tf_op jit(solution)/shard_map/ppermute | solution.py:221
  76.6 14.3 %all-gather = f32[1792,128]{1,0:T(8,128)} all-gather(f32[896,128]{1,0:T(8,128)S(1)} %pad_maximum_fusion), channel_id=2, replica_groups={{0,1},{2,3},{4,5},{6,7},{8,9},{10,11},{12,13},{14,15},{16,17},{18,19},{..., dimensions={0}, use_global_device_ids=true | all-gather | bytes 1376256 | tf_op jit(solution)/shard_map/all_gather | solution.py:235
  90.9 13.6 %factor.1 = (f32[256,128]{1,0:T(8,128)}, f32[256,384]{1,0:T(8,128)}) custom-call(f32[2,896,128]{2,1,0:T(8,128)} %bitcast.17), custom_call_target="tpu_custom_call" | custom-call | tf_op jit(solution)/shard_map/factor/pallas_call | solution.py:121
  104.5 0.0 all-to-all-done.4.y_ref
  104.5 0.0 copy-start
  104.5 0.9 copy-done
  105.4 2.7 %finish.1 = f32[2,512,128]{2,1,0:T(8,128)} custom-call(f32[256,128]{1,0:T(8,128)} %get-tuple-element.7.panel_ref, f32[256,384]{1,0:T(8,128)} %get-tuple-element.8.gain_ref, f32[8,192,128]{2,1,0:T(8,128)} %copy-done, f32[2,512,128]{2,1,0:T(8,128)} %bitcast.18), custom_call_target="tpu_custom_call" | custom-call | tf_op jit(solution)/shard_map/finish/pallas_call | solution.py:188
  (10 shorter events, 0.1 us)
Async XLA Ops:
  0.0 0.9 slice-start
  32.6 9.2 %all-to-all-start.2 = ((f32[4,96,128]{2,1,0:T(8,128)}), f32[4,96,128]{2,1,0:T(8,128)S(1)}, u32[]{:S(2)}, u32[]{:S(2)}) async-start(f32[4,96,128]{2,1,0:T(8,128)} %broadcast_in_dim.10), calls=%async_computation.2 | async-start | bytes 393216 | tf_op jit(solution)/shard_map/all_to_all | solution.py:199
  41.8 0.7 copy-start.2
  42.5 11.9 %all-to-all-start.3 = ((f32[8,48,128]{2,1,0:T(8,128)}), f32[8,48,128]{2,1,0:T(8,128)S(1)}, u32[]{:S(2)}, u32[]{:S(2)}) async-start(f32[8,48,128]{2,1,0:T(8,128)} %broadcast_in_dim.22), calls=%async_computation.3 | async-start | bytes 393216 | tf_op jit(solution)/shard_map/all_to_all | solution.py:199
  47.8 10.2 %copy-start.1 = (f32[2,128,4,128]{3,2,1,0:T(4,128)S(1)}, f32[2,128,4,128]{3,2,1,0:T(4,128)}, u32[]{:S(2)}) copy-start(f32[2,128,4,128]{3,2,1,0:T(4,128)} %param.1) | copy-start | bytes 1572868
  54.5 50.0 %all-to-all-start.4 = ((f32[8,192,128]{2,1,0:T(8,128)}), f32[8,192,128]{2,1,0:T(8,128)S(1)}, u32[]{:S(2)}, u32[]{:S(2)}) async-start(f32[8,192,128]{2,1,0:T(8,128)} %shard_map.17), calls=%async_computation.4 | async-start | bytes 1572864 | tf_op jit(solution)/shard_map/all_to_all | solution.py:237
  58.1 0.7 collective-permute-start
  58.9 0.7 collective-permute-start.1
  59.6 17.0 %collective-permute-start.2 = (f32[256,128]{1,0:T(8,128)S(1)}, f32[256,128]{1,0:T(8,128)S(1)}, u32[]{:S(2)}, u32[]{:S(2)}) collective-permute-start(f32[256,128]{1,0:T(8,128)S(1)} %broadcast_select_fusion.1), channel_id=1, source_target_pairs={{0,2},{1,3},{2,0},{4,6},{5,7},{6,4},{8,10},{9,11},{10,8},{12,14},{... | collective-permute-start | bytes 393224 | tf_op jit(solution)/shard_map/ppermute | solution.py:221
  104.5 0.9 copy-start
